TPU v7x, 32 devices: a whole 2x2x4 slice. The times are simulated.
32 devices in a mesh: shard: 2 (over x), ctx: 4 (over z), tp: 4 (over y, core).
Axes of the slice: x: 2, y: 2, z: 4, core: 2. Of those that a mesh axis runs over, the one named last changes fastest.
Arguments:
- hidden_in: bfloat16 [4, 2048, 768], P('shard', 'ctx'), may hold values from -6 to 6
- segment_ids: int32 [4, 2048], P('shard'), may hold values from 0 to 7, never falling along the last dimension, each value on 1 to 1024 neighbouring positions
- qkv_weight: float32 [768, 3, 768], P('shard', None, 'tp'), may hold values from -0.21875 to 0.21875
- qv_bias: float32 [2, 768], P(None, 'tp'), may hold values from -3 to 3
- out_weight: float32 [768, 768], P('tp', 'shard'), may hold values from -1.75 to 1.75
- out_bias: float32 [768], P('shard'), may hold values from -3 to 3
- first_gain: float32 [768], P('shard'), may hold values from 0.5 to 1.5
- first_shift: float32 [768], P('shard'), may hold values from -3 to 3
- inner_weight: float32 [768, 3072], P('shard', 'tp'), may hold values from -0.21875 to 0.21875
- inner_bias: float32 [3072], P('tp'), may hold values from -3 to 3
- outer_weight: float32 [3072, 768], P('tp', 'shard'), may hold values from -0.109375 to 0.109375
- outer_bias: float32 [768], P('shard'), may hold values from -3 to 3
- second_gain: float32 [768], P('shard'), may hold values from 0.5 to 1.5
- second_shift: float32 [768], P('shard'), may hold values from -3 to 3
- cotangent: bfloat16 [4, 2048, 768], P('shard', 'ctx'), may hold values from -6 to 6
Outputs:
- output: bfloat16 [4, 2048, 768], P('shard', 'ctx')
- grad_hidden: bfloat16 [4, 2048, 768], P('shard', 'ctx')
- grad_qkv_weight: float32 [768, 3, 768], P('shard', None, 'tp')
- grad_qv_bias: float32 [2, 768], P(None, 'tp')
- grad_out_weight: float32 [768, 768], P('tp', 'shard')
- grad_out_bias: float32 [768], P('shard')
- grad_first_gain: float32 [768], P('shard')
- grad_first_shift: float32 [768], P('shard')
- grad_inner_weight: float32 [768, 3072], P('shard', 'tp')
- grad_inner_bias: float32 [3072], P('tp')
- grad_outer_weight: float32 [3072, 768], P('tp', 'shard')
- grad_outer_bias: float32 [768], P('shard')
- grad_second_gain: float32 [768], P('shard')
- grad_second_shift: float32 [768], P('shard')
Inputs may be any that keep to these rules, and one draw needn't show every extreme that they name: `segment_ids`: within a row ids never fall; each document has 1 to 1024 tokens and one has exactly 1024.
All inputs are finite; a program needn't handle non-finite values.
Results may differ from a plain program's by a relative error of at most 0.014.
The roundings to bfloat16 on the way count: a program that leaves them out, or rounds other values in their place, can miss the bound.
Values may be sent and summed in bfloat16 or wider, within the bound.
No kernel may reach another device: no remote copies, remote signals or barrier semaphores. Data moves between devices by JAX's collectives and lax.ppermute only.
A program may use at most 128 MiB of HBM per device.

v0:
```python
import jax
import jax.numpy as jnp
from jax import lax
from jax.sharding import PartitionSpec as P

HEAD_DIM = 64


EPSILON = 1e-12
NEGATIVE = -1e30


def layer_norm(summed, gain_vec, shift_vec):
    average = jnp.mean(summed, -1, keepdims=True)
    centered = summed - average
    variance = jnp.mean(centered * centered, -1, keepdims=True)
    return centered * lax.rsqrt(variance + EPSILON) * gain_vec + shift_vec


def exact_gelu(values_in):
    return jax.nn.gelu(values_in, approximate=False)


def masked_scores(query_row, key_row, query_seg, key_seg):
    scores = jnp.einsum(
        "hid,hjd->hij", query_row, key_row, preferred_element_type=jnp.float32
    ) * HEAD_DIM ** (-0.5)
    allowed = query_seg[:, None] == key_seg[None, :]
    return jnp.where(allowed[None], scores, NEGATIVE)


def attend_forward(query_row, key_row, value_row, query_seg, key_seg):
    scores = masked_scores(query_row, key_row, query_seg, key_seg)
    largest = jnp.max(scores, -1, keepdims=True)
    weights_exp = jnp.exp(scores - largest)
    totals = jnp.sum(weights_exp, -1, keepdims=True)
    probability = (weights_exp / totals).astype(jnp.bfloat16)
    mixed = jnp.einsum("hij,hjd->hid", probability, value_row, preferred_element_type=jnp.float32)
    return (mixed, largest + jnp.log(totals))


def probs_and_grads(query_row, key_row, value_row, query_seg, key_seg, logsum, grad_mixed):
    scores = masked_scores(query_row, key_row, query_seg, key_seg)
    probs = jnp.exp(scores - logsum)
    grad_probs = jnp.einsum(
        "hid,hjd->hij", grad_mixed, value_row, preferred_element_type=jnp.float32
    )
    return (probs, grad_probs)


def attend_backward(query_row, key_row, value_row, query_seg, key_seg, logsum, grad_mixed):
    probs, grad_probs = probs_and_grads(
        query_row, key_row, value_row, query_seg, key_seg, logsum, grad_mixed
    )
    weighted = jnp.sum(probs * grad_probs, -1, keepdims=True)
    grad_scores = (probs * (grad_probs - weighted) * HEAD_DIM ** (-0.5)).astype(jnp.bfloat16)
    grad_query = jnp.einsum(
        "hij,hjd->hid", grad_scores, key_row, preferred_element_type=jnp.float32
    )
    grad_key = jnp.einsum(
        "hij,hid->hjd", grad_scores, query_row, preferred_element_type=jnp.float32
    )
    grad_value = jnp.einsum(
        "hij,hid->hjd", probs.astype(jnp.bfloat16), grad_mixed, preferred_element_type=jnp.float32
    )
    return (grad_query, grad_key, grad_value)


def body(
    hidden_in,
    segment_ids,
    qkv_weight,
    qv_bias,
    out_weight,
    out_bias,
    first_gain,
    first_shift,
    inner_weight,
    inner_bias,
    outer_weight,
    outer_bias,
    second_gain,
    second_shift,
    cotangent,
):
    rows_dev, tok_dev, width = hidden_in.shape
    local_cols = qkv_weight.shape[2]
    heads_here = local_cols // HEAD_DIM
    flat_rows = rows_dev * tok_dev
    vectors = jnp.stack(
        [out_bias, first_gain, first_shift, outer_bias, second_gain, second_shift]
    ).astype(jnp.bfloat16)
    qkv_low = qkv_weight.astype(jnp.bfloat16)
    out_low = out_weight.astype(jnp.bfloat16)
    inner_low = inner_weight.astype(jnp.bfloat16)
    outer_low = outer_weight.astype(jnp.bfloat16)
    full_qkv, full_out, full_inner, full_outer, full_vectors = (
        lax.all_gather(qkv_low, "shard", axis=0, tiled=True),
        lax.all_gather(out_low, "shard", axis=1, tiled=True),
        lax.all_gather(inner_low, "shard", axis=0, tiled=True),
        lax.all_gather(outer_low, "shard", axis=1, tiled=True),
        lax.all_gather(vectors, "shard", axis=1, tiled=True),
    )
    vector_vals = full_vectors.astype(jnp.float32)
    tokens = hidden_in.reshape(flat_rows, width)
    qkv_heads = full_qkv.reshape(width, 3, heads_here, HEAD_DIM)
    projected = jnp.einsum(
        "rtd,dchk->crhtk", hidden_in, qkv_heads, preferred_element_type=jnp.float32
    )
    bias_heads = qv_bias.reshape(2, heads_here, HEAD_DIM)
    query_heads = (projected[0] + bias_heads[0][None, :, None, :]).astype(jnp.bfloat16)
    key_heads = projected[1].astype(jnp.bfloat16)
    value_heads = (projected[2] + bias_heads[1][None, :, None, :]).astype(jnp.bfloat16)
    all_keys, all_values = (
        lax.all_gather(key_heads, "ctx", axis=2, tiled=True),
        lax.all_gather(value_heads, "ctx", axis=2, tiled=True),
    )
    offset = lax.axis_index("ctx") * tok_dev
    query_segs = lax.dynamic_slice_in_dim(segment_ids, offset, tok_dev, 1)

    def forward_row(sliced):
        query_row, key_row, value_row, query_seg, key_seg = sliced
        return attend_forward(query_row, key_row, value_row, query_seg, key_seg)

    mixed, logsum = lax.map(
        forward_row, (query_heads, all_keys, all_values, query_segs, segment_ids)
    )
    mixed_low = mixed.astype(jnp.bfloat16)
    out_heads = full_out.reshape(heads_here, HEAD_DIM, width)
    head_part = jnp.einsum(
        "rhtk,hkd->rtd", mixed_low, out_heads, preferred_element_type=jnp.float32
    ).reshape(flat_rows, width)
    first_sum = tokens.astype(jnp.float32) + lax.psum(head_part, "tp") + vector_vals[0]
    first_norm, first_pull = jax.vjp(layer_norm, first_sum, vector_vals[1], vector_vals[2])
    norm_low = first_norm.astype(jnp.bfloat16)
    activation = jnp.dot(norm_low, full_inner, preferred_element_type=jnp.float32) + inner_bias
    gelu_out, gelu_pull = jax.vjp(exact_gelu, activation)
    gelu_low = gelu_out.astype(jnp.bfloat16)
    unit_part = jnp.dot(gelu_low, full_outer, preferred_element_type=jnp.float32)
    second_sum = first_norm + lax.psum(unit_part, "tp") + vector_vals[3]
    result, second_pull = jax.vjp(layer_norm, second_sum, vector_vals[4], vector_vals[5])
    output = result.astype(jnp.bfloat16).reshape(rows_dev, tok_dev, width)
    back_qkv, back_out, back_inner, back_outer = (
        lax.all_gather(qkv_low, "shard", axis=0, tiled=True),
        lax.all_gather(out_low, "shard", axis=1, tiled=True),
        lax.all_gather(inner_low, "shard", axis=0, tiled=True),
        lax.all_gather(outer_low, "shard", axis=1, tiled=True),
    )
    grad_second, grad_gain_two, grad_shift_two = second_pull(
        cotangent.reshape(flat_rows, width).astype(jnp.float32)
    )
    grad_outer_bias = jnp.sum(grad_second, 0)
    second_low = grad_second.astype(jnp.bfloat16)
    grad_outer = jnp.einsum("tf,td->fd", gelu_low, second_low, preferred_element_type=jnp.float32)
    grad_gelu = jnp.einsum("td,fd->tf", second_low, back_outer, preferred_element_type=jnp.float32)
    grad_act = gelu_pull(grad_gelu)[0]
    grad_inner_bias = jnp.sum(grad_act, 0)
    act_low = grad_act.astype(jnp.bfloat16)
    grad_inner = jnp.einsum("td,tf->df", norm_low, act_low, preferred_element_type=jnp.float32)
    norm_part = jnp.einsum("tf,df->td", act_low, back_inner, preferred_element_type=jnp.float32)
    back_norm = lax.psum(norm_part, "tp")
    grad_first, grad_gain_one, grad_shift_one = first_pull(grad_second + back_norm)
    grad_out_bias = jnp.sum(grad_first, 0)
    first_low = grad_first.astype(jnp.bfloat16).reshape(rows_dev, tok_dev, width)
    grad_out = jnp.einsum(
        "rhtk,rtd->hkd", mixed_low, first_low, preferred_element_type=jnp.float32
    ).reshape(local_cols, width)
    back_out_heads = back_out.reshape(heads_here, HEAD_DIM, width)
    grad_mixed = jnp.einsum(
        "rtd,hkd->rhtk", first_low, back_out_heads, preferred_element_type=jnp.float32
    ).astype(jnp.bfloat16)

    def backward_row(sliced):
        query_row, key_row, value_row, query_seg, key_seg, row_logsum, row_grad = sliced
        return attend_backward(
            query_row, key_row, value_row, query_seg, key_seg, row_logsum, row_grad
        )

    grad_query, grad_keys, grad_values = lax.map(
        backward_row,
        (query_heads, all_keys, all_values, query_segs, segment_ids, logsum, grad_mixed),
    )
    grad_key_local, grad_value_local = (
        lax.psum_scatter(grad_keys, "ctx", scatter_dimension=2, tiled=True),
        lax.psum_scatter(grad_values, "ctx", scatter_dimension=2, tiled=True),
    )
    grad_qv = jnp.stack(
        [
            jnp.sum(grad_query, (0, 2)).reshape(local_cols),
            jnp.sum(grad_value_local, (0, 2)).reshape(local_cols),
        ]
    )
    projected_grad = jnp.stack([grad_query, grad_key_local, grad_value_local]).astype(jnp.bfloat16)
    grad_qkv = jnp.einsum(
        "rtd,crhtk->dchk", hidden_in, projected_grad, preferred_element_type=jnp.float32
    ).reshape(width, 3, local_cols)
    back_qkv_heads = back_qkv.reshape(width, 3, heads_here, HEAD_DIM)
    input_part = jnp.einsum(
        "crhtk,dchk->rtd", projected_grad, back_qkv_heads, preferred_element_type=jnp.float32
    ).reshape(flat_rows, width)
    grad_hidden = (
        (grad_first + lax.psum(input_part, "tp"))
        .astype(jnp.bfloat16)
        .reshape(rows_dev, tok_dev, width)
    )
    grad_vectors = jnp.stack(
        [
            grad_out_bias,
            grad_gain_one,
            grad_shift_one,
            grad_outer_bias,
            grad_gain_two,
            grad_shift_two,
        ]
    )
    grad_qv, grad_inner_bias = lax.psum((grad_qv, grad_inner_bias), ("shard", "ctx"))
    owned = (
        lax.psum_scatter(grad_qkv, "shard", scatter_dimension=0, tiled=True),
        lax.psum_scatter(grad_out, "shard", scatter_dimension=1, tiled=True),
        lax.psum_scatter(grad_inner, "shard", scatter_dimension=0, tiled=True),
        lax.psum_scatter(grad_outer, "shard", scatter_dimension=1, tiled=True),
        lax.psum_scatter(grad_vectors, "shard", scatter_dimension=1, tiled=True),
    )
    pieces = lax.psum((owned[0], owned[1], owned[2], owned[3], owned[4]), "ctx")
    piece_qkv, piece_out, piece_inner, piece_outer, piece_vectors = pieces
    return (
        output,
        grad_hidden,
        piece_qkv,
        grad_qv,
        piece_out,
        piece_vectors[0],
        piece_vectors[1],
        piece_vectors[2],
        piece_inner,
        grad_inner_bias,
        piece_outer,
        piece_vectors[3],
        piece_vectors[4],
        piece_vectors[5],
    )


def solution(mesh):
    in_specs = (
        P("shard", "ctx", None),
        P("shard", None),
        P("shard", None, "tp"),
        P(None, "tp"),
        P("tp", "shard"),
        P("shard"),
        P("shard"),
        P("shard"),
        P("shard", "tp"),
        P("tp"),
        P("tp", "shard"),
        P("shard"),
        P("shard"),
        P("shard"),
        P("shard", "ctx", None),
    )
    out_specs = (
        P("shard", "ctx", None),
        P("shard", "ctx", None),
        P("shard", None, "tp"),
        P(None, "tp"),
        P("tp", "shard"),
        P("shard"),
        P("shard"),
        P("shard"),
        P("shard", "tp"),
        P("tp"),
        P("tp", "shard"),
        P("shard"),
        P("shard"),
        P("shard"),
    )
    return jax.shard_map(body, mesh=mesh, in_specs=in_specs, out_specs=out_specs, check_vma=False)
```

profile of v0, /device:TPU:0, one launch (start us, length us, event | category | flops | bytes accessed | tf_op | source)
XLA Modules:
  0.0 1000.5 jit_solution(5112832982896725825)
XLA Ops:
  9.3 13.8 %all_gather.25 = bf16[768,3,192]{0,2,1:T(8,128)(2,1)S(1)} all-gather(bf16[384,3,192]{0,2,1:T(8,128)(2,1)S(1)} %convert_element_type.83), channel_id=1, replica_groups=mesh['shard'=2,'ctx'=4,'tp'=4] {'shard'}, dimensions={0}, use_global_device_ids=true | all-gather | bytes 1327104 | tf_op jit(solution)/shard_map/all_gather | solution.py:98
  36.0 30.1 %all-gather.12.cloned.1.call-done = bf16[1,2,3,2048,64]{3,4,1,2,0:T(8,128)(2,1)} async-done(((bf16[1,2,3,512,64]{3,4,1,2,0:T(8,128)(2,1)}), bf16[1,2,3,2048,64]{3,4,1,2,0:T(8,128)(2,1)}) %all-gather.12.cloned.1.call-update) | async-done | bytes 1572880 | tf_op jit(solution)/shard_map/all_gather | solution.py:115
  67.6 36.5 %all-gather.6.cloned.1.call-done = bf16[2,3,2048,64]{2,3,0,1:T(8,128)(2,1)} async-done(((bf16[2,3,512,64]{2,3,0,1:T(8,128)(2,1)}), bf16[2,3,2048,64]{2,3,0,1:T(8,128)(2,1)}) %all-gather.6.cloned.1.call-update) | async-done | bytes 1572880 | tf_op jit(solution)/shard_map/all_gather | solution.py:116
  105.6 44.4 %while.28 = (s32[]{:T(128)}, bf16[2,3,512,64]{2,3,1,0:T(8,128)(2,1)}, f32[2,3,512,1]{2,1,3,0:T(4,128)}, s32[2,512]{1,0:T(2,128)}, s32[2,2048]{1,0:T(2,128)S(1)},...) while((s32[]{:T(128)}, ...), condition=%wide.region_3.4_spmd.clone, body=%wide.region_0.3_spmd.sunk.clone | while | flops 844102144 | bytes 47442136 | solution.py:125
  107.0 5.9 fusion.195
  112.9 6.8 fusion.196
  119.7 6.7 fusion.197
  129.2 5.9 fusion.195
  135.1 6.8 fusion.196
  141.9 6.7 fusion.197
  163.8 58.3 %all-reduce.8.cloned.1.call-done = f32[1024,768]{1,0:T(8,128)} async-done(((f32[1024,768]{1,0:T(8,128)}), f32[1024,768]{1,0:T(8,128)}) %all-reduce.8.cloned.1.call-update) | async-done | bytes 3145744 | tf_op jit(solution)/shard_map/psum | solution.py:133
  227.3 11.0 %multiply_convert_fusion.1 = (bf16[1024,768]{1,0:T(8,128)(2,1)}, f32[1024,768]{1,0:T(8,128)}, f32[1024,768]{1,0:T(8,128)}) fusion(f32[768]{0:T(1024)} %param.28, bf16[768,768]{1,0:T(8,128)(2,1)} %all-gather.8.cloned.1.call-done, f32[1024,768]{1,0:T(8,128)S(1)} %get-tuple-element.232, f32[768]{0:T(1024)} %get-tuple-element.167, ...), kind=kOutput, calls=%fused_computation.100 | convolution fusion | flops 1263796224 | bytes 12207104 | tf_op jit(solution)/shard_map/dot_general | solution.py:136
  243.1 68.6 %all-reduce.10.cloned.1.call-done = f32[1024,768]{1,0:T(8,128)} async-done(((f32[1024,768]{1,0:T(8,128)}), f32[1024,768]{1,0:T(8,128)}) %all-reduce.10.cloned.1.call-update) | async-done | bytes 3145744 | tf_op jit(solution)/shard_map/psum | solution.py:140
  329.6 68.6 %all-reduce.12.cloned.1.call-done = f32[1024,768]{1,0:T(8,128)} async-done(((f32[1024,768]{1,0:T(8,128)}), f32[1024,768]{1,0:T(8,128)}) %all-reduce.12.cloned.1.call-update) | async-done | bytes 3145744 | tf_op jit(solution)/shard_map/psum | solution.py:161
  407.5 113.6 %while.29 = (s32[]{:T(128)}, f32[2,3,512,64]{2,3,1,0:T(8,128)}, f32[2,3,2048,64]{2,3,0,1:T(8,128)}, f32[2,3,2048,64]{2,3,0,1:T(8,128)}, s32[2,512]{1,0:T(2,128)S...) while((s32[]{:T(128)}, f32[2,3,512,64]{2,3,1,0:T(8,128)}, ...), condition=%wide.region_17.18_spmd.clone, body=%wide.region_15.17_spmd.sunk.clone | while | flops 2096110592 | bytes 208100528 | solution.py:179
  415.4 6.3 fusion.208
  421.7 20.7 %fusion.210 = f32[2,3,512,64]{2,3,1,0:T(8,128)} fusion(f32[2,3,512,64]{2,3,1,0:T(8,128)} %get-tuple-element.448, s32[]{:T(128)S(6)} %copy.103, f32[3,512,2048]{2,1,0:T(8,128)} %fusion.208, f32[3,512,2048]{2,1,0:T(8,128)} %copy-done, f32[3,512]{1,0:T(4,128)S(1)} %dynamic-slice_bitcast_fusion.3, ...), kind=kOutput, calls=%fused_computation.47.clone.1.clone | convolution fusion | flops 437259776 | bytes 53625856 | tf_op jit(solution)/shard_map/while/body/eval_jaxpr/hij,hjd->hid/dot_general | solution.py:57
  442.5 21.8 %fusion.211 = f32[2,3,2048,64]{2,3,0,1:T(8,128)} fusion(f32[2,3,2048,64]{2,3,0,1:T(8,128)} %get-tuple-element.449, s32[]{:T(128)S(6)} %copy.103, f32[3,512,2048]{2,1,0:T(8,128)} %fusion.208, f32[3,512,2048]{2,1,0:T(8,128)} %copy-done, f32[3,512]{1,0:T(4,128)S(1)} %dynamic-slice_bitcast_fusion.3, ...), kind=kOutput, calls=%fused_computation.44.clone.1.clone | convolution fusion | flops 437259776 | bytes 54215680 | tf_op jit(solution)/shard_map/while/body/eval_jaxpr/hij,hid->hjd/dot_general | solution.py:60
  472.0 6.3 fusion.208
  478.3 20.7 %fusion.210 = f32[2,3,512,64]{2,3,1,0:T(8,128)} fusion(f32[2,3,512,64]{2,3,1,0:T(8,128)} %get-tuple-element.448, s32[]{:T(128)S(6)} %copy.103, f32[3,512,2048]{2,1,0:T(8,128)} %fusion.208, f32[3,512,2048]{2,1,0:T(8,128)} %copy-done, f32[3,512]{1,0:T(4,128)S(1)} %dynamic-slice_bitcast_fusion.3, ...), kind=kOutput, calls=%fused_computation.47.clone.1.clone | convolution fusion | flops 437259776 | bytes 53625856 | tf_op jit(solution)/shard_map/while/body/eval_jaxpr/hij,hjd->hid/dot_general | solution.py:57
  499.1 21.9 %fusion.211 = f32[2,3,2048,64]{2,3,0,1:T(8,128)} fusion(f32[2,3,2048,64]{2,3,0,1:T(8,128)} %get-tuple-element.449, s32[]{:T(128)S(6)} %copy.103, f32[3,512,2048]{2,1,0:T(8,128)} %fusion.208, f32[3,512,2048]{2,1,0:T(8,128)} %copy-done, f32[3,512]{1,0:T(4,128)S(1)} %dynamic-slice_bitcast_fusion.3, ...), kind=kOutput, calls=%fused_computation.44.clone.1.clone | convolution fusion | flops 437259776 | bytes 54215680 | tf_op jit(solution)/shard_map/while/body/eval_jaxpr/hij,hid->hjd/dot_general | solution.py:60
  535.6 46.2 %reduce-scatter.10.cloned.1.call-done = f32[2,3,512,64]{2,3,0,1:T(8,128)} async-done(((f32[2,3,2048,64]{2,3,0,1:T(8,128)}), f32[2,3,512,64]{2,3,0,1:T(8,128)}) %reduce-scatter.10.cloned.1.call-update) | async-done | bytes 786448 | tf_op jit(solution)/shard_map/reduce_scatter | solution.py:185
  583.3 61.1 %reduce-scatter.8.cloned.1.call-done = f32[2,3,512,64]{2,3,0,1:T(8,128)} async-done(((f32[2,3,2048,64]{2,3,0,1:T(8,128)}), f32[2,3,512,64]{2,3,0,1:T(8,128)}) %reduce-scatter.8.cloned.1.call-update) | async-done | bytes 786448 | tf_op jit(solution)/shard_map/reduce_scatter | solution.py:184
  654.6 8.0 reduce-scatter.14.cloned.1.call-done
  662.6 37.1 %reduce-scatter.20.cloned.1.call-done = f32[768,384]{1,0:T(8,128)} async-done(((f32[768,768]{1,0:T(8,128)}), f32[768,384]{1,0:T(8,128)}) %reduce-scatter.20.cloned.1.call-update) | async-done | bytes 1179664 | tf_op jit(solution)/shard_map/reduce_scatter | solution.py:221
  699.7 36.9 %reduce-scatter.18.cloned.1.call-done = f32[384,768]{1,0:T(8,128)} async-done(((f32[768,768]{1,0:T(8,128)}), f32[384,768]{1,0:T(8,128)}) %reduce-scatter.18.cloned.1.call-update) | async-done | bytes 1179664 | tf_op jit(solution)/shard_map/reduce_scatter | solution.py:220
  736.6 30.6 %reduce-scatter.12.cloned.1.call-done = f32[384,3,192]{0,2,1:T(8,128)} async-done(((f32[768,3,192]{0,2,1:T(8,128)}), f32[384,3,192]{0,2,1:T(8,128)}) %reduce-scatter.12.cloned.1.call-update) | async-done | bytes 884752 | tf_op jit(solution)/shard_map/reduce_scatter | solution.py:218
  768.6 11.3 %reduce-scatter.16.cloned.1.call-done = f32[6,384]{1,0:T(8,128)} async-done(((f32[6,768]{1,0:T(8,128)}), f32[6,384]{1,0:T(8,128)}) %reduce-scatter.16.cloned.1.call-update) | async-done | bytes 9232 | tf_op jit(solution)/shard_map/reduce_scatter | solution.py:222
  779.8 19.3 %psum.84 = f32[6,384]{1,0:T(8,128)S(1)} all-reduce(f32[6,384]{1,0:T(8,128)} %reduce-scatter.16.cloned.1.call-done), channel_id=1, replica_groups=mesh['shard'=2,'ctx'=4,'tp'=4] {'ctx'}, use_global_device_ids=true, to_apply=%region_35.36 | all-reduce | flops 2304 | bytes 18432 | tf_op jit(solution)/shard_map/psum | solution.py:224
  799.9 18.3 %all-reduce = (f32[2,192]{1,0:T(2,128)}, f32[768]{0:T(1024)}) all-reduce(f32[2,192]{1,0:T(2,128)S(1)} %pad_maximum_fusion.2, f32[768]{0:T(1024)S(1)} %copy-done.50), channel_id=1, replica_groups=mesh['shard'=2,'ctx'=4,'tp'=4] {'shard','ctx'}, use_global_device_ids=true, to_apply=%region_25.26 | all-reduce | flops 1152 | bytes 9216 | tf_op jit(solution)/shard_map/psum | solution.py:216
  818.2 32.5 %all-reduce.14.cloned.1.call-done = f32[1024,768]{1,0:T(8,128)} async-done(((f32[1024,768]{1,0:T(8,128)}), f32[1024,768]{1,0:T(8,128)}) %all-reduce.14.cloned.1.call-update) | async-done | bytes 3145744 | tf_op jit(solution)/shard_map/psum | solution.py:202
  854.0 133.1 %all-reduce.16.cloned.1.call-done = (f32[384,3,192]{0,2,1:T(8,128)}, f32[192,384]{1,0:T(8,128)}, f32[384,768]{1,0:T(8,128)}, f32[768,384]{1,0:T(8,128)}) async-done(((f32[384,3,192]{0,2,1:T(8,128)}, f32[192,384]{1,0:T(8,128)}, f32[384,768]{1,0:T(8,128)}, f32[768,384]{1,0:T(8,128)}), (f32[384,3,192]{0,2,1:T(8,128)}, f32[192,384]{1,0:T(8,128)}, f32[384,768]{1,0:T(8,128)}, ...) | async-done | bytes 3538960 | tf_op jit(solution)/shard_map/psum | solution.py:224
  (281 shorter events, 125.3 us)
Async XLA Ops:
  8.0 58.0 %all-gather.12.cloned.1.call-start = ((), (), s32[]{:S(2)}) async-start(), calls=%async_computation.21 | async-start | bytes 1966080 | tf_op jit(solution)/shard_map/all_gather | solution.py:115
  26.6 8.0 copy-start.23
  27.4 76.7 %all-gather.6.cloned.1.call-start = ((), (), s32[]{:S(2)}) async-start(), calls=%async_computation.7 | async-start | bytes 1966080 | tf_op jit(solution)/shard_map/all_gather | solution.py:116
  28.5 193.5 %all-reduce.8.cloned.1.call-start = ((), (), s32[]{:S(2)}) async-start(), calls=%async_computation.8 | async-start | bytes 6291456 | tf_op jit(solution)/shard_map/psum | solution.py:133
  112.9 6.8 copy-start.14
  119.7 6.7 copy-start.29
  135.1 6.8 copy-start.14
  141.9 6.7 copy-start.29
  154.6 72.6 %all-gather.8.cloned.1.call-start = ((), (), s32[]{:S(2)}) async-start(), calls=%async_computation.9 | async-start | bytes 1769472 | tf_op jit(solution)/shard_map/all_gather | solution.py:100
  157.0 81.2 %all-gather.10.cloned.1.call-start = ((), (), s32[]{:S(2)}) async-start(), calls=%async_computation.10 | async-start | bytes 1769472 | tf_op jit(solution)/shard_map/all_gather | solution.py:101
  158.0 153.8 %all-reduce.10.cloned.1.call-start = ((), (), s32[]{:S(2)}) async-start(), calls=%async_computation.11 | async-start | bytes 6291456 | tf_op jit(solution)/shard_map/psum | solution.py:140
  224.9 178.2 %copy-start.1 = (f32[1024,768]{1,0:T(8,128)}, f32[1024,768]{1,0:T(8,128)S(1)}, u32[]{:S(2)}) copy-start(f32[1024,768]{1,0:T(8,128)S(1)} %get-tuple-element.232) | copy-start | bytes 9437188
  243.1 155.1 %all-reduce.12.cloned.1.call-start = ((), (), s32[]{:S(2)}) async-start(), calls=%async_computation.12 | async-start | bytes 6291456 | tf_op jit(solution)/shard_map/psum | solution.py:161
  329.5 252.3 %reduce-scatter.10.cloned.1.call-start = ((), (), s32[]{:S(2)}) async-start(), calls=%async_computation.14 | async-start | bytes 3932160 | tf_op jit(solution)/shard_map/reduce_scatter | solution.py:185
  410.2 5.2 copy-start
  466.8 5.2 copy-start
  521.2 123.3 %reduce-scatter.8.cloned.1.call-start = ((), (), s32[]{:S(2)}) async-start(), calls=%async_computation.13 | async-start | bytes 3932160 | tf_op jit(solution)/shard_map/reduce_scatter | solution.py:184
  521.9 140.7 %reduce-scatter.14.cloned.1.call-start = ((), (), s32[]{:S(2)}) async-start(), calls=%async_computation.17 | async-start | bytes 884736 | tf_op jit(solution)/shard_map/reduce_scatter | solution.py:219
  523.9 5.7 copy-start.2
  523.9 5.7 copy-start.28
  523.9 5.7 copy-start.33
  523.9 5.7 copy-start.35
  524.0 5.7 copy-start.47
  524.0 175.7 %reduce-scatter.20.cloned.1.call-start = ((), (), s32[]{:S(2)}) async-start(), calls=%async_computation.20 | async-start | bytes 3538944 | tf_op jit(solution)/shard_map/reduce_scatter | solution.py:221
  529.5 207.1 %reduce-scatter.18.cloned.1.call-start = ((), (), s32[]{:S(2)}) async-start(), calls=%async_computation.19 | async-start | bytes 3538944 | tf_op jit(solution)/shard_map/reduce_scatter | solution.py:220
  534.4 232.8 %reduce-scatter.12.cloned.1.call-start = ((), (), s32[]{:S(2)}) async-start(), calls=%async_computation.16 | async-start | bytes 2654208 | tf_op jit(solution)/shard_map/reduce_scatter | solution.py:218
  649.6 130.2 %reduce-scatter.16.cloned.1.call-start = ((), (), s32[]{:S(2)}) async-start(), calls=%async_computation.18 | async-start | bytes 36864 | tf_op jit(solution)/shard_map/reduce_scatter | solution.py:222
  651.0 199.7 %all-reduce.14.cloned.1.call-start = ((), (), s32[]{:S(2)}) async-start(), calls=%async_computation.15 | async-start | bytes 6291456 | tf_op jit(solution)/shard_map/psum | solution.py:202
  654.5 145.4 %copy-start.50 = (f32[768]{0:T(1024)S(1)}, f32[768]{0:T(1024)}, u32[]{:S(2)}) copy-start(f32[768]{0:T(1024)} %get-tuple-element.244) | copy-start | bytes 9220
  654.5 196.2 %copy-start.4 = (f32[1024,768]{1,0:T(8,128)S(1)}, f32[1024,768]{1,0:T(8,128)}, u32[]{:S(2)}) copy-start(f32[1024,768]{1,0:T(8,128)} %copy-done.3) | copy-start | bytes 9437188
  654.5 196.2 %copy-start.37 = (f32[1024]{0:T(1024)S(1)}, f32[1024]{0:T(1024)}, u32[]{:S(2)}) copy-start(f32[1024]{0:T(1024)} %copy-done.36) | copy-start | bytes 12292
  654.5 332.6 %all-reduce.16.cloned.1.call-start = ((), (), s32[]{:S(2)}) async-start(), calls=%async_computation.22 | async-start | bytes 7077888 | tf_op jit(solution)/shard_map/psum | solution.py:224
  (54 other events, 143.0 us)
Sparse Core Ops, SparseCore 0:
  27.5 38.4 all-gather.11
  68.2 35.8 all-gather.5
  154.7 67.2 all-reduce.7
  243.2 68.5 all-reduce.9
  329.6 68.5 all-reduce.11
  521.3 60.4 reduce-scatter.9
  584.1 60.2 reduce-scatter.7
  647.3 15.2 reduce-scatter.13
  664.8 34.7 reduce-scatter.19
  701.8 34.7 reduce-scatter.17
  738.9 28.2 reduce-scatter.11
  769.8 9.9 reduce-scatter.15
  782.2 68.4 all-reduce.13
  853.2 133.9 all-reduce.15
Sparse Core Ops, SparseCore 1:
  157.2 21.4 all-gather.7
  180.7 22.6 all-gather.9
where the time goes:
time: 1010 us; the launch traced here: 1000 us
  waiting for transfers between devices  660 us (65%)
  matrix products  184 us (18%)
  blocking collectives  62.2 us (6%)
  other arithmetic  49.1 us (5%)
  local copies, waits for them, and re-layouts  27.7 us (3%)
  between operations  16.5 us (2%)
    psum x1, waiting for transfers between devices, body(): pieces = lax.psum((owned[0], owned[1], owned[2], owned[3], owned[4]), 'ctx')  133 us
    psum x1, waiting for transfers between devices, body(): second_sum = first_norm + lax.psum(unit_part, 'tp') + vector_vals[3]  68.6 us
    psum x1, waiting for transfers between devices, body(): back_norm = lax.psum(norm_part, 'tp')  68.6 us
    reduce_scatter x1, waiting for transfers between devices, body(): lax.psum_scatter(grad_keys, 'ctx', scatter_dimension=2, tiled=True)  61.1 us
    psum x1, waiting for transfers between devices, body(): lax.psum(head_part, 'tp')  58.3 us
    reduce_scatter x1, waiting for transfers between devices, body(): lax.psum_scatter(grad_values, 'ctx', scatter_dimension=2, tiled=True)  46.2 us
    dot_general x2, matrix products, attend_backward(): jnp.einsum('hij,hid->hjd', grad_scores, query_row, preferred_element_type...  43.6 us
    dot_general x2, matrix products, attend_backward(): jnp.einsum('hij,hjd->hid', grad_scores, key_row, preferred_element_type=j...  41.5 us
  transfers between devices with their start and end apart: 16, of which 14 were waited for; matrix products, arithmetic and copies ran while one was open for 5% of the time, Pallas kernels for 0%

commit v1 on v0

v1 whole, which is shorter than its diff:
```python
import functools

import jax
import jax.numpy as jnp
from jax import lax
from jax.experimental import pallas as pl
from jax.experimental.pallas import tpu as pltpu
from jax.sharding import PartitionSpec as P

HEAD_DIM = 64
LONGEST = 1024
EPSILON = 1e-12
NEGATIVE = -1e30
BF = jnp.bfloat16
F32 = jnp.float32


def dot(a, b):
    return jnp.dot(a, b, preferred_element_type=F32)


def dot_tn(a, b):
    return lax.dot_general(a, b, (((0,), (0,)), ((), ())), preferred_element_type=F32)


def dot_nt(a, b):
    return lax.dot_general(a, b, (((1,), (1,)), ((), ())), preferred_element_type=F32)


def head_stack(tile, first, heads):
    row = lax.broadcasted_iota(jnp.int32, tile.shape, 0)
    parts = []
    for h in range(heads):
        start = first + h * HEAD_DIM
        parts.append(jnp.where((row >= start) & (row < start + HEAD_DIM), tile, jnp.zeros_like(tile)))
    return jnp.concatenate(parts, 1)


def head_rows(tile, first, heads):
    col = lax.broadcasted_iota(jnp.int32, tile.shape, 1)
    parts = []
    for h in range(heads):
        start = first + h * HEAD_DIM
        parts.append(jnp.where((col >= start) & (col < start + HEAD_DIM), tile, jnp.zeros_like(tile)))
    return jnp.concatenate(parts, 0)


def load_blocks(kv_refs, kvb, sem, tok):
    copies = [
        pltpu.make_async_copy(ref, kvb.at[pl.ds(i * tok, tok)], sem.at[i])
        for i, ref in enumerate(kv_refs)
    ]
    for copy in copies:
        copy.start()
    for copy in copies:
        copy.wait()


def forward_kernel(slots, heads, tq, tk, rng, q_ref, qseg_ref, kseg_ref, *rest):
    kv_refs = rest[:slots]
    o_ref, lse_ref, kvb, st, acc, sem = rest[slots:]
    tok = q_ref.shape[0]
    wide = q_ref.shape[1]
    load_blocks(kv_refs, kvb, sem, tok)
    vfirst = 2 * heads * HEAD_DIM - wide
    voff = wide - heads * HEAD_DIM
    for t in range(tok // tq):
        lo, hi = rng[3 * t], rng[3 * t + 1]
        qs = pl.multiple_of(rng[3 * t + 2], tq)
        q3t = head_stack(q_ref[pl.ds(qs, tq), :].T, 0, heads)
        qseg = qseg_ref[t]

        def scan_scores(j, top, q3t=q3t, qseg=qseg):
            at = pl.multiple_of(j * tk, tk)
            scores = dot(kvb[pl.ds(at, tk), :wide], q3t)
            scores = jnp.where(kseg_ref[pl.ds(at, tk), :] == qseg, scores, NEGATIVE)
            st[pl.ds(at, tk), :] = scores
            return jnp.maximum(top, jnp.max(scores.reshape(tk // 8, 8, heads * tq), 0))

        top8 = lax.fori_loop(lo, hi, scan_scores, jnp.full((8, heads * tq), NEGATIVE, F32))
        top = jnp.max(top8, 0, keepdims=True)
        acc[...] = jnp.zeros_like(acc)

        def scan_values(j, total, top=top):
            at = pl.multiple_of(j * tk, tk)
            weights = jnp.exp(st[pl.ds(at, tk), :] - top)
            acc[...] += dot_tn(kvb[pl.ds(at, tk), vfirst:], weights.astype(BF))
            return total + jnp.sum(weights.reshape(tk // 8, 8, heads * tq), 0)

        total8 = lax.fori_loop(lo, hi, scan_values, jnp.zeros((8, heads * tq), F32))
        total = jnp.sum(total8, 0, keepdims=True)
        lse_ref[t] = top + jnp.log(total)
        inv = 1.0 / total
        pieces = [jnp.zeros((voff, tq), F32)]
        for h in range(heads):
            rows = slice(voff + h * HEAD_DIM, voff + (h + 1) * HEAD_DIM)
            cols = slice(h * tq, (h + 1) * tq)
            pieces.append(acc[rows, cols] * inv[:, cols])
        o_ref[t * tq : (t + 1) * tq, :] = jnp.concatenate(pieces, 0).T.astype(BF)


def backward_kernel(slots, heads, tq, tk, rng, q_ref, qseg_ref, kseg_ref, o_ref, do_ref, lse_ref, *rest):
    kv_refs = rest[:slots]
    dq_ref, bias_ref = rest[slots : slots + 2]
    dkv_refs = rest[slots + 2 : 2 * slots + 2]
    kvb, dkv, dqt, sem = rest[2 * slots + 2 :]
    tok = q_ref.shape[0]
    wide = q_ref.shape[1]
    load_blocks(kv_refs, kvb, sem, tok)
    vfirst = 2 * heads * HEAD_DIM - wide
    voff = wide - heads * HEAD_DIM
    dkv[...] = jnp.zeros_like(dkv)
    bias = jnp.zeros((1, wide), F32)
    for t in range(tok // tq):
        lo, hi = rng[3 * t], rng[3 * t + 1]
        qs = pl.multiple_of(rng[3 * t + 2], tq)
        q = q_ref[pl.ds(qs, tq), :]
        do = do_ref[t * tq : (t + 1) * tq, :]
        o = o_ref[t * tq : (t + 1) * tq, :]
        q3t = head_stack(q.T, 0, heads)
        q3 = head_rows(q, 0, heads)
        do3t = head_stack(do.T, voff, heads)
        do3 = head_rows(do, voff, heads)
        prod = (do.astype(F32) * o.astype(F32)).T
        delta = jnp.concatenate(
            [
                jnp.sum(prod[voff + h * HEAD_DIM : voff + (h + 1) * HEAD_DIM], 0, keepdims=True)
                for h in range(heads)
            ],
            1,
        )
        qseg = qseg_ref[t]
        lse = lse_ref[t]
        dqt[...] = jnp.zeros_like(dqt)

        def scan_blocks(j, carry, q3t=q3t, q3=q3, do3t=do3t, do3=do3, delta=delta, qseg=qseg, lse=lse):
            at = pl.multiple_of(j * tk, tk)
            k = kvb[pl.ds(at, tk), :wide]
            v = kvb[pl.ds(at, tk), vfirst:]
            scores = dot(k, q3t)
            same = kseg_ref[pl.ds(at, tk), :] == qseg
            probs = jnp.where(same, jnp.exp(scores - lse), 0.0)
            grad = (probs * (dot(v, do3t) - delta)).astype(BF)
            dkv[pl.ds(at, tk), :wide] += dot(grad, q3)
            dkv[pl.ds(at, tk), vfirst:] += dot(probs.astype(BF), do3)
            dqt[...] += dot_tn(k, grad)
            return carry

        lax.fori_loop(lo, hi, scan_blocks, 0)
        pieces = []
        for h in range(heads):
            pieces.append(dqt[h * HEAD_DIM : (h + 1) * HEAD_DIM, h * tq : (h + 1) * tq])
        pieces.append(jnp.zeros((wide - heads * HEAD_DIM, tq), F32))
        dq = jnp.concatenate(pieces, 0).T * HEAD_DIM**-0.5
        bias = bias + jnp.sum(dq, 0, keepdims=True)
        dq_ref[pl.ds(qs, tq), :] = dq.astype(BF)
    bias_ref[...] = bias
    for i, ref in enumerate(dkv_refs):
        ref[...] = dkv[i * tok : (i + 1) * tok, :].astype(BF)


def make_attention(slots, heads, tok, wide, packed):
    tq = tok // 2
    tk = tq
    vmem = pl.BlockSpec(memory_space=pltpu.VMEM)
    smem = pl.BlockSpec(memory_space=pltpu.SMEM)
    hbm = pl.BlockSpec(memory_space=pl.ANY)
    pairs = 3 * heads * tok * slots * tok * wide
    params = pltpu.CompilerParams(vmem_limit_bytes=48 << 20)
    forward = pl.pallas_call(
        functools.partial(forward_kernel, slots, heads, tq, tk),
        out_shape=(
            jax.ShapeDtypeStruct((tok, wide), BF),
            jax.ShapeDtypeStruct((2, 1, heads * tq), F32),
        ),
        in_specs=[smem, vmem, vmem, vmem] + [hbm] * slots,
        out_specs=(vmem, vmem),
        scratch_shapes=[
            pltpu.VMEM((slots * tok, packed), BF),
            pltpu.VMEM((slots * tok, heads * tq), F32),
            pltpu.VMEM((wide, heads * tq), F32),
            pltpu.SemaphoreType.DMA((slots,)),
        ],
        cost_estimate=pl.CostEstimate(
            flops=pairs, transcendentals=heads * tok * slots * tok, bytes_accessed=slots * tok * packed * 2
        ),
        compiler_params=params,
        name="attend_forward",
    )
    backward = pl.pallas_call(
        functools.partial(backward_kernel, slots, heads, tq, tk),
        out_shape=(
            jax.ShapeDtypeStruct((tok, wide), BF),
            jax.ShapeDtypeStruct((1, wide), F32),
        )
        + tuple(jax.ShapeDtypeStruct((tok, packed), BF) for _ in range(slots)),
        in_specs=[smem, vmem, vmem, vmem, vmem, vmem, vmem] + [hbm] * slots,
        out_specs=(vmem,) * (slots + 2),
        scratch_shapes=[
            pltpu.VMEM((slots * tok, packed), BF),
            pltpu.VMEM((slots * tok, packed), F32),
            pltpu.VMEM((wide, heads * tq), F32),
            pltpu.SemaphoreType.DMA((slots,)),
        ],
        cost_estimate=pl.CostEstimate(
            flops=3 * pairs,
            transcendentals=heads * tok * slots * tok,
            bytes_accessed=slots * tok * packed * 4,
        ),
        compiler_params=params,
        name="attend_backward",
    )
    return forward, backward


def make_body(n_shard, n_ctx, n_tp):
    bits = [1 << i for i in range(n_tp.bit_length() - 1)]

    def exchange(value, axis, size, bit):
        return lax.ppermute(value, axis, [(i, i ^ bit) for i in range(size)])

    def shift(value, step):
        pairs = [(i, i + step) for i in range(n_ctx) if 0 <= i + step < n_ctx]
        return lax.ppermute(value, "ctx", pairs)

    def ctx_sum(value):
        if n_ctx & (n_ctx - 1):
            return lax.psum(value, "ctx")
        ci = lax.axis_index("ctx")
        steps = [1 << i for i in range(n_ctx.bit_length() - 1)]
        cur = value
        for bit in steps:
            half = cur.shape[0] // 2
            up = (ci // bit) % 2
            send = lax.dynamic_slice_in_dim(cur, (1 - up) * half, half, 0).astype(BF)
            keep = lax.dynamic_slice_in_dim(cur, up * half, half, 0)
            cur = keep + exchange(send, "ctx", n_ctx, bit).astype(F32)
        cur = cur.astype(BF)
        for bit in reversed(steps):
            other = exchange(cur, "ctx", n_ctx, bit)
            up = (ci // bit) % 2
            cur = jnp.where(
                up == 0, jnp.concatenate([cur, other], 0), jnp.concatenate([other, cur], 0)
            )
        return cur.astype(F32)

    def body(
        hidden_in,
        segment_ids,
        qkv_weight,
        qv_bias,
        out_weight,
        out_bias,
        first_gain,
        first_shift,
        inner_weight,
        inner_bias,
        outer_weight,
        outer_bias,
        second_gain,
        second_shift,
        cotangent,
    ):
        rows, tok, width = hidden_in.shape
        part = width // n_shard
        cols = qkv_weight.shape[2]
        heads = cols // HEAD_DIM
        units = inner_weight.shape[1]
        wide = -(-cols // 128) * 128
        pad = wide - cols
        packed = 2 * cols
        half = tok // 2
        si = lax.axis_index("shard")
        ci = lax.axis_index("ctx")
        core = lax.axis_index("tp") % 2
        reach = min(n_ctx - 1, 1 + (LONGEST - 2) // tok)
        slots = 2 * reach + 1
        attend_fwd, attend_bwd = make_attention(slots, heads, tok, wide, packed)

        def rolled(value, axis):
            if n_shard == 2:
                first = lax.slice_in_dim(value, 0, part, axis=axis)
                second = lax.slice_in_dim(value, part, width, axis=axis)
                return jnp.where(si == 0, value, jnp.concatenate([second, first], axis))
            return jnp.roll(value, -si * part, axis)

        def unrolled(value, axis):
            if n_shard == 2:
                return rolled(value, axis)
            return jnp.roll(value, si * part, axis)

        def gathered(own, axis):
            if n_shard == 2:
                return jnp.concatenate([own, exchange(own, "shard", 2, 1)], axis)
            return rolled(lax.all_gather(own, "shard", axis=axis, tiled=True), axis)

        def shard_sum(make, axis):
            if n_shard == 2:
                send = make(part, width).astype(BF)
                return make(0, part) + exchange(send, "shard", 2, 1).astype(F32)
            whole = unrolled(make(0, width), axis)
            return lax.psum_scatter(whole, "shard", scatter_dimension=axis, tiled=True)

        def own_half(value):
            return lax.dynamic_slice_in_dim(value, core * half, half, 0)

        def other_half(value):
            return lax.dynamic_slice_in_dim(value, (1 - core) * half, half, 0)

        def tp_sum(own, send):
            total = own + exchange(send.astype(BF), "tp", n_tp, 1).astype(F32)
            for bit in bits[1:]:
                total = total.astype(BF)
                total = total.astype(F32) + exchange(total, "tp", n_tp, bit).astype(F32)
            return total

        def both_halves(own):
            return jnp.concatenate([own, exchange(own, "tp", n_tp, 1)], 0)

        def in_order(pair):
            first, second = pair[:half], pair[half:]
            return jnp.where(core == 0, pair, jnp.concatenate([second, first], 0))

        qkv_low = qkv_weight.astype(BF)
        kv_own = qkv_low[:, 1:].reshape(part, packed)
        q_own = jnp.pad(qkv_low[:, 0], ((0, 0), (0, pad)))
        w_kv = gathered(kv_own, 0)
        w_q = gathered(q_own, 0)
        vec_own = jnp.stack(
            [out_bias, first_gain, first_shift, outer_bias, second_gain, second_shift]
        ).astype(BF)
        vec_own = jnp.pad(vec_own, ((0, 10), (0, 0)))
        wo_vec = gathered(jnp.concatenate([out_weight.astype(BF), vec_own], 0), 1)
        w_out = jnp.concatenate([jnp.zeros((pad, width), BF), wo_vec[:cols]], 0)
        vectors = wo_vec[cols : cols + 6].astype(F32)
        w_in = gathered(inner_weight.astype(BF), 0)
        w_outer = gathered(outer_weight.astype(BF), 1)

        x = rolled(hidden_in, 2)
        cot = rolled(cotangent, 2)

        before = jnp.full((rows, reach * tok), -1, jnp.int32)
        after = jnp.full((rows, reach * tok), 1 << 20, jnp.int32)
        padded = jnp.concatenate([before, segment_ids, after], 1)
        key_seg = lax.dynamic_slice_in_dim(padded, ci * tok, slots * tok, 1)
        q_seg = lax.dynamic_slice_in_dim(segment_ids, ci * tok, tok, 1)
        q_seg = q_seg.reshape(rows, 2, half)
        q_seg = jnp.where(core == 0, q_seg, q_seg[:, ::-1])
        low = jnp.sum(key_seg[:, None, :] < q_seg[:, :, :1], -1) // half
        high = (jnp.sum(key_seg[:, None, :] <= q_seg[:, :, -1:], -1) + half - 1) // half
        begin = jnp.broadcast_to(jnp.stack([core * half, (1 - core) * half])[None], (rows, 2))
        ranges = jnp.stack([low, high, begin], -1).reshape(rows, 6).astype(jnp.int32)
        q_seg3 = jnp.tile(q_seg[:, :, None, :], (1, 1, 1, heads))
        key_col = key_seg[:, :, None]

        v_bias = jnp.concatenate([jnp.zeros((cols,), F32), qv_bias[1]])
        q_bias = jnp.pad(qv_bias[0], (0, pad))

        def blocks_of(own):
            left, right = [own], [own]
            for _ in range(reach):
                left.append(shift(left[-1], 1))
                right.append(shift(right[-1], -1))
            return left[:0:-1] + [own] + right[1:]

        kv = [blocks_of((dot(x[r], w_kv) + v_bias).astype(BF)) for r in range(rows)]
        q = [
            ((dot(x[r], w_q) + q_bias).astype(BF) * jnp.asarray(HEAD_DIM**-0.5, BF))
            for r in range(rows)
        ]

        def normed(summed):
            average = jnp.mean(summed, -1, keepdims=True)
            centered = summed - average
            variance = jnp.mean(centered * centered, -1, keepdims=True)
            scale = lax.rsqrt(variance + EPSILON)
            return centered * scale, scale

        def norm_back(grad, gain, hat, scale):
            inner = grad * gain
            return scale * (
                inner
                - jnp.mean(inner, -1, keepdims=True)
                - hat * jnp.mean(inner * hat, -1, keepdims=True)
            )

        bo, g1, s1, bd, g2, s2 = [vectors[i] for i in range(6)]
        saved = []
        for r in range(rows):
            o, lse = attend_fwd(ranges[r], q[r], q_seg3[r], key_col[r], *kv[r])
            total = tp_sum(dot(o[:half], w_out), dot(o[half:], w_out))
            h1 = own_half(x[r]).astype(F32) + total + bo
            hat1, scale1 = normed(h1)
            y1 = hat1 * g1 + s1
            y1b = both_halves(y1.astype(BF))
            a = dot(y1b, w_in) + inner_bias
            cdf = 0.5 * (1.0 + lax.erf(a * (0.5**0.5)))
            u = (a * cdf).astype(BF)
            slope = (cdf + a * jnp.exp(-0.5 * a * a) * 0.3989422804014327).astype(BF)
            total = tp_sum(dot(u[:half], w_outer), dot(u[half:], w_outer))
            h2 = y1 + total + bd
            hat2, scale2 = normed(h2)
            saved.append((o, lse, hat1, scale1, y1b, u, slope, hat2, scale2))

        outputs = []
        d_vec = jnp.zeros((6, width), F32)
        d_bi = jnp.zeros((units,), F32)
        d_bq = jnp.zeros((wide,), F32)
        d_bv = jnp.zeros((cols,), F32)
        d2b, d1b, dab, dqs, dkvs, dh1s = [], [], [], [], [], []
        for r in range(rows):
            o, lse, hat1, scale1, y1b, u, slope, hat2, scale2 = saved[r]
            c = own_half(cot[r]).astype(F32)
            result = (hat2 * g2 + s2).astype(BF)
            outputs.append(in_order(both_halves(unrolled(result, 1))))
            dh2 = norm_back(c, g2, hat2, scale2)
            dh2b = both_halves(dh2.astype(BF))
            du = dot_nt(dh2b, w_outer)
            da = du * slope.astype(F32)
            d_bi = d_bi + jnp.sum(da, 0)
            da_low = da.astype(BF)
            total = tp_sum(dot_nt(da_low[:half], w_in), dot_nt(da_low[half:], w_in))
            dy1 = dh2 + total
            dh1 = norm_back(dy1, g1, hat1, scale1)
            dh1b = both_halves(dh1.astype(BF))
            d_vec = d_vec + jnp.stack(
                [
                    jnp.sum(dh1, 0),
                    jnp.sum(dy1 * hat1, 0),
                    jnp.sum(dy1, 0),
                    jnp.sum(dh2, 0),
                    jnp.sum(c * hat2, 0),
                    jnp.sum(c, 0),
                ]
            )
            do = dot_nt(dh1b, w_out).astype(BF)
            res = attend_bwd(ranges[r], q[r], q_seg3[r], key_col[r], o, do, lse, *kv[r])
            dq, bias = res[:2]
            parts = res[2:]
            d_bq = d_bq + bias[0]
            carry_right = carry_left = None
            for d in range(reach, 0, -1):
                right, left = parts[reach + d], parts[reach - d]
                if carry_right is not None:
                    right = (right.astype(F32) + carry_right.astype(F32)).astype(BF)
                    left = (left.astype(F32) + carry_left.astype(F32)).astype(BF)
                carry_right, carry_left = shift(right, 1), shift(left, -1)
            dkv = parts[reach].astype(F32)
            if carry_right is not None:
                dkv = dkv + carry_right.astype(F32) + carry_left.astype(F32)
            d_bv = d_bv + jnp.sum(dkv[:, cols:], 0)
            d2b.append(dh2b)
            d1b.append(dh1b)
            dab.append(da_low)
            dqs.append(dq)
            dkvs.append(dkv.astype(BF))
            dh1s.append(dh1)

        hidden_grads = []
        for r in range(rows):
            total = tp_sum(
                dot_nt(own_half(dqs[r]), w_q) + dot_nt(own_half(dkvs[r]), w_kv),
                dot_nt(other_half(dqs[r]), w_q) + dot_nt(other_half(dkvs[r]), w_kv),
            )
            grad = unrolled((dh1s[r] + total).astype(BF), 1)
            hidden_grads.append(in_order(both_halves(grad)))

        every = range(rows)

        def total_of(terms):
            return functools.reduce(lambda p, q: p + q, terms)

        g_outer = shard_sum(lambda a, b: total_of(dot_tn(saved[r][5], d2b[r][:, a:b]) for r in every), 1)
        g_in = shard_sum(lambda a, b: total_of(dot_tn(saved[r][4][:, a:b], dab[r]) for r in every), 0)
        g_out = shard_sum(
            lambda a, b: total_of(dot_tn(saved[r][0], d1b[r][:, a:b]) for r in every)[pad:], 1
        )
        g_q = shard_sum(lambda a, b: total_of(dot_tn(x[r][:, a:b], dqs[r]) for r in every)[:, :cols], 0)
        g_kv = shard_sum(lambda a, b: total_of(dot_tn(x[r][:, a:b], dkvs[r]) for r in every), 0)
        g_outer = ctx_sum(g_outer)
        g_in = ctx_sum(g_in)
        g_out = ctx_sum(g_out)
        g_q = ctx_sum(g_q)
        g_kv = ctx_sum(g_kv)
        grad_qkv = jnp.concatenate([g_q[:, None], g_kv.reshape(part, 2, cols)], 1)

        d_vec = d_vec + exchange(d_vec, "tp", n_tp, 1)
        small = jnp.concatenate([d_bi, d_bq[:cols], d_bv])
        if n_shard == 2:
            send = jnp.concatenate([d_vec[:, part:].reshape(-1), small])
            flat = jnp.concatenate([d_vec[:, :part].reshape(-1), small]) + exchange(send, "shard", 2, 1)
        else:
            vec = lax.psum_scatter(unrolled(d_vec, 1), "shard", scatter_dimension=1, tiled=True)
            flat = jnp.concatenate([vec.reshape(-1), lax.psum(small, "shard")])
        if n_ctx & (n_ctx - 1):
            flat = lax.psum(flat, "ctx")
        else:
            for bit in [1 << i for i in range(n_ctx.bit_length() - 1)]:
                flat = flat + exchange(flat, "ctx", n_ctx, bit)
        vec = flat[: 6 * part].reshape(6, part)
        small = flat[6 * part :]
        return (
            jnp.stack(outputs),
            jnp.stack(hidden_grads),
            grad_qkv,
            small[units:].reshape(2, cols),
            g_out,
            vec[0],
            vec[1],
            vec[2],
            g_in,
            small[:units],
            g_outer,
            vec[3],
            vec[4],
            vec[5],
        )

    return body


def solution(mesh):
    body = make_body(mesh.shape["shard"], mesh.shape["ctx"], mesh.shape["tp"])
    in_specs = (
        P("shard", "ctx", None),
        P("shard", None),
        P("shard", None, "tp"),
        P(None, "tp"),
        P("tp", "shard"),
        P("shard"),
        P("shard"),
        P("shard"),
        P("shard", "tp"),
        P("tp"),
        P("tp", "shard"),
        P("shard"),
        P("shard"),
        P("shard"),
        P("shard", "ctx", None),
    )
    out_specs = (
        P("shard", "ctx", None),
        P("shard", "ctx", None),
        P("shard", None, "tp"),
        P(None, "tp"),
        P("tp", "shard"),
        P("shard"),
        P("shard"),
        P("shard"),
        P("shard", "tp"),
        P("tp"),
        P("tp", "shard"),
        P("shard"),
        P("shard"),
        P("shard"),
    )
    return jax.shard_map(body, mesh=mesh, in_specs=in_specs, out_specs=out_specs, check_vma=False)
```

time: 1010 us -> 407 us (0.40)
  waiting for transfers between devices: 660 us -> 136 us
  matrix products: 184 us -> 54.4 us
  starting transfers between devices: 0.67 us -> 116 us
  blocking collectives: 62.2 us -> 0 us
  Pallas kernels: 0 us -> 30.9 us
  between operations: 16.5 us -> 3.14 us
  other arithmetic: 49.1 us -> 38.2 us
    psum x5 -> x0, waiting for transfers between devices: 361 us -> none  [the longest x1 133 us: body(): pieces = lax.psum((owned[0], owned[1], owned[2], owned[3], owned[4]), 'ctx')]
    reduce_scatter x7 -> x0, waiting for transfers between devices: 231 us -> none  [the longest x1 61.1 us: body(): lax.psum_scatter(grad_keys, 'ctx', scatter_dimension=2, tiled=True)]
    ppermute x0 -> x76, waiting for transfers between devices: none -> 136 us  [the longest x60 126 us: exchange(): return lax.ppermute(value, axis, [(i, i ^ bit) for i in range(size)])]
    dot_general x26 -> x50, matrix products: 184 us -> 54.4 us  [the longest x16 22.6 us: dot_nt(): lax.dot_general(a, b, (((1,), (1,)), ((), ())), preferred_element_type=F32)]
    ppermute x0 -> x76, starting transfers between devices: none -> 116 us  [the longest x60 65.2 us: exchange(): return lax.ppermute(value, axis, [(i, i ^ bit) for i in range(size)])]
    all_gather x4 -> x0, waiting for transfers between devices: 66.6 us -> none  [the longest x1 36.5 us: body(): lax.all_gather(value_heads, 'ctx', axis=2, tiled=True)]
    psum x2 -> x0, blocking collectives: 37.6 us -> none  [the longest x1 19.3 us: body(): pieces = lax.psum((owned[0], owned[1], owned[2], owned[3], owned[4]), 'ctx')]
    pallas_call x0 -> x4, Pallas kernels: none -> 30.9 us  [the longest x2 17.9 us: body(): res = attend_bwd(ranges[r], q[r], q_seg3[r], key_col[r], o, do, lse, *kv[r])]
  transfers between devices with their start and end apart: 16 -> 76, of which waited for: 14 -> 32; matrix products, arithmetic and copies ran while one was open for 5% -> 24% of each run, Pallas kernels for 0% -> 8%
where the time goes in v1:
time: 407 us; the launch traced here: 400 us
  waiting for transfers between devices  136 us (33%)
  starting transfers between devices  116 us (29%)
  matrix products  54.4 us (13%)
  other arithmetic  38.2 us (9%)
  Pallas kernels  30.9 us (8%)
  local copies, waits for them, and re-layouts  20.9 us (5%)
    ppermute x60, waiting for transfers between devices, exchange(): return lax.ppermute(value, axis, [(i, i ^ bit) for i in range(size)])  126 us
    ppermute x60, starting transfers between devices, exchange(): return lax.ppermute(value, axis, [(i, i ^ bit) for i in range(size)])  65.2 us
    ppermute x16, starting transfers between devices, shift(): return lax.ppermute(value, 'ctx', pairs)  51.2 us
    dot_general x16, matrix products, dot_nt(): lax.dot_general(a, b, (((1,), (1,)), ((), ())), preferred_element_type=F32)  22.6 us
    pallas_call x2, Pallas kernels, body(): res = attend_bwd(ranges[r], q[r], q_seg3[r], key_col[r], o, do, lse, *kv[r])  17.9 us
    dot_general x14, matrix products, dot(): return jnp.dot(a, b, preferred_element_type=F32)  17.3 us
    dot_general x20, matrix products, dot_tn(): lax.dot_general(a, b, (((0,), (0,)), ((), ())), preferred_element_type=F32)  14.4 us
    pallas_call x2, Pallas kernels, body(): o, lse = attend_fwd(ranges[r], q[r], q_seg3[r], key_col[r], *kv[r])  13 us
  transfers between devices with their start and end apart: 76, of which 32 were waited for; matrix products, arithmetic and copies ran while one was open for 24% of the time, Pallas kernels for 8%

profile of v1, /device:TPU:0, one launch (start us, length us, event | category | flops | bytes accessed | tf_op | source)
XLA Modules:
  0.0 399.5 jit_solution(18365405409210350468)
XLA Ops:
  14.7 9.7 %collective-permute-done.1 = bf16[384,384]{0,1:T(8,128)(2,1)S(1)} collective-permute-done((bf16[384,384]{0,1:T(8,128)(2,1)S(1)}, bf16[384,384]{0,1:T(8,128)(2,1)S(1)}, u32[]{:S(2)}, u32[]{:S(2)}) %collective-permute-start.1) | collective-permute-done | bytes 294944 | tf_op jit(solution)/shard_map/ppermute | solution.py:220
  27.0 5.3 %collective-permute-start.2 = (bf16[512,384]{1,0:T(8,128)(2,1)}, bf16[512,384]{1,0:T(8,128)(2,1)}, u32[]{:S(2)}, u32[]{:S(2)}) collective-permute-start(bf16[512,384]{1,0:T(8,128)(2,1)} %fusion.16.rest_2_), channel_id=1, source_target_pairs={{0,4},{4,8},{8,12},{1,5},{5,9},{9,13},{2,6},{6,10},{10,14},{3,7},{... | collective-permute-start | bytes 1179656 | tf_op jit(solution)/shard_map/ppermute | solution.py:224
  38.3 4.6 %collective-permute-start.15 = (bf16[512,384]{1,0:T(8,128)(2,1)S(1)}, bf16[512,384]{1,0:T(8,128)(2,1)S(1)}, u32[]{:S(2)}, u32[]{:S(2)}) collective-permute-start(bf16[512,384]{1,0:T(8,128)(2,1)S(1)} %fusion.19.rest_2_), channel_id=1, source_target_pairs={{0,4},{4,8},{8,12},{1,5},{5,9},{9,13},{2,6},{6,10},{10,14},{3,7},{... | collective-permute-start | bytes 1179656 | tf_op jit(solution)/shard_map/ppermute | solution.py:224
  44.2 4.6 %collective-permute-start.3 = (bf16[512,384]{1,0:T(8,128)(2,1)}, bf16[512,384]{1,0:T(8,128)(2,1)S(1)}, u32[]{:S(2)}, u32[]{:S(2)}) collective-permute-start(bf16[512,384]{1,0:T(8,128)(2,1)} %collective-permute-done.2.rest_1_), channel_id=1, source_target_pairs={{0,4},{4,8},{8,12},{1,5},{5,9},{9,13},{2,6},{6,10},{10,14},{3,7},{... | collective-permute-start | bytes 1179656 | tf_op jit(solution)/shard_map/ppermute | solution.py:224
  53.0 4.6 %collective-permute-start.16 = (bf16[512,384]{1,0:T(8,128)(2,1)S(1)}, bf16[512,384]{1,0:T(8,128)(2,1)S(1)}, u32[]{:S(2)}, u32[]{:S(2)}) collective-permute-start(bf16[512,384]{1,0:T(8,128)(2,1)S(1)} %collective-permute-done.15.rest_1_), channel_id=1, source_target_pairs={{0,4},{4,8},{8,12},{1,5},{5,9},{9,13},{2,6},{6,10},{10,14},{3,7},{... | collective-permute-start | bytes 1179656 | tf_op jit(solution)/shard_map/ppermute | solution.py:224
  60.9 7.5 %attend_forward.2 = (bf16[512,256]{1,0:T(8,128)(2,1)S(1)}, f32[2,1,768]{2,1,0:T(1,128)S(1)}) custom-call(s32[6]{0:T(128)S(1)} %squeeze.18.rng, bf16[512,256]{1,0:T(8,128)(2,1)S(1)} %fusion.33.q_ref, s32[2,1,768]{2,1,0:T(1,128)S(1)} %tile.16.qseg_ref, s32[2560,1]{1,0:T(8,128)S(1)} %copy.73.kseg_ref, bf16[512,384]{1,0:T(8,128)(2,1)S(1)} %collective-permute-done.3.rest_0_, ...), custom_call_target="tpu_custom_call" | custom-call | flops 3019898880 | bytes 1966080 | tf_op jit(solution)/shard_map/attend_forward/pallas_call | solution.py:390
  68.8 5.6 %attend_forward.3 = (bf16[512,256]{1,0:T(8,128)(2,1)S(1)}, f32[2,1,768]{2,1,0:T(1,128)S(1)}) custom-call(s32[6]{0:T(128)S(1)} %squeeze.24.rng, bf16[512,256]{1,0:T(8,128)(2,1)S(1)} %fusion.32.q_ref, s32[2,1,768]{2,1,0:T(1,128)S(1)} %tile.17.qseg_ref, s32[2560,1]{1,0:T(8,128)S(1)} %copy.76.kseg_ref, bf16[512,384]{1,0:T(8,128)(2,1)S(1)} %collective-permute-done.16.rest_0_, ...), custom_call_target="tpu_custom_call" | custom-call | flops 3019898880 | bytes 1966080 | tf_op jit(solution)/shard_map/attend_forward/pallas_call | solution.py:390
  87.7 7.5 %collective-permute-done.20 = bf16[256,768]{1,0:T(8,128)(2,1)} collective-permute-done((bf16[256,768]{1,0:T(8,128)(2,1)S(1)}, bf16[256,768]{1,0:T(8,128)(2,1)}, u32[]{:S(2)}, u32[]{:S(2)}) %collective-permute-start.20) | collective-permute-done | bytes 393248 | tf_op jit(solution)/shard_map/ppermute | solution.py:220
  104.9 9.9 %collective-permute-done.11 = bf16[768,384]{1,0:T(8,128)(2,1)S(1)} collective-permute-done((bf16[768,384]{1,0:T(8,128)(2,1)S(1)}, bf16[768,384]{1,0:T(8,128)(2,1)S(1)}, u32[]{:S(2)}, u32[]{:S(2)}) %collective-permute-start.11) | collective-permute-done | bytes 589856 | tf_op jit(solution)/shard_map/ppermute | solution.py:220
  129.9 4.4 %collective-permute-done.23 = bf16[256,768]{1,0:T(8,128)(2,1)} collective-permute-done((bf16[256,768]{1,0:T(8,128)(2,1)}, bf16[256,768]{1,0:T(8,128)(2,1)}, u32[]{:S(2)}, u32[]{:S(2)}) %collective-permute-start.23) | collective-permute-done | bytes 393248 | tf_op jit(solution)/shard_map/ppermute | solution.py:220
  134.3 7.9 %collective-permute-done.13 = bf16[256,768]{1,0:T(8,128)(2,1)} collective-permute-done((bf16[256,768]{1,0:T(8,128)(2,1)}, bf16[256,768]{1,0:T(8,128)(2,1)}, u32[]{:S(2)}, u32[]{:S(2)}) %collective-permute-start.13) | collective-permute-done | bytes 393248 | tf_op jit(solution)/shard_map/ppermute | solution.py:220
  172.2 3.9 collective-permute-done.66
  176.7 6.2 %collective-permute-start.67 = (bf16[192,768]{1,0:T(8,128)(2,1)S(1)}, bf16[192,768]{1,0:T(8,128)(2,1)}, u32[]{:S(2)}, u32[]{:S(2)}) collective-permute-start(bf16[192,768]{1,0:T(8,128)(2,1)S(1)} %dynamic-slice_convert_fusion.1), channel_id=1, source_target_pairs={{0,4},{4,0},{8,12},{12,8},{1,5},{5,1},{9,13},{13,9},{2,6},{6,2},{1... | collective-permute-start | bytes 884744 | tf_op jit(solution)/shard_map/ppermute | solution.py:220
  182.9 5.3 %collective-permute-done.71 = bf16[768,384]{1,0:T(8,128)(2,1)S(1)} collective-permute-done((bf16[768,384]{1,0:T(8,128)(2,1)S(1)}, bf16[768,384]{1,0:T(8,128)(2,1)S(1)}, u32[]{:S(2)}, u32[]{:S(2)}) %collective-permute-start.71) | collective-permute-done | bytes 589856 | tf_op jit(solution)/shard_map/ppermute | solution.py:220
  196.0 6.2 %collective-permute-start.72 = (bf16[384,384]{1,0:T(8,128)(2,1)S(1)}, bf16[384,384]{1,0:T(8,128)(2,1)S(1)}, u32[]{:S(2)}, u32[]{:S(2)}) collective-permute-start(bf16[384,384]{1,0:T(8,128)(2,1)S(1)} %dynamic-slice_convert_fusion), channel_id=1, source_target_pairs={{0,4},{4,0},{8,12},{12,8},{1,5},{5,1},{9,13},{13,9},{2,6},{6,2},{1... | collective-permute-start | bytes 884744 | tf_op jit(solution)/shard_map/ppermute | solution.py:220
  206.3 6.3 %collective-permute-done.72 = bf16[384,384]{1,0:T(8,128)(2,1)S(1)} collective-permute-done((bf16[384,384]{1,0:T(8,128)(2,1)S(1)}, bf16[384,384]{1,0:T(8,128)(2,1)S(1)}, u32[]{:S(2)}, u32[]{:S(2)}) %collective-permute-start.72) | collective-permute-done | bytes 294944 | tf_op jit(solution)/shard_map/ppermute | solution.py:220
  213.1 7.5 %collective-permute-done.68 = bf16[96,768]{1,0:T(8,128)(2,1)S(1)} collective-permute-done((bf16[96,768]{1,0:T(8,128)(2,1)S(1)}, bf16[96,768]{1,0:T(8,128)(2,1)S(1)}, u32[]{:S(2)}, u32[]{:S(2)}) %collective-permute-start.68) | collective-permute-done | bytes 147488 | tf_op jit(solution)/shard_map/ppermute | solution.py:220
  225.1 6.1 %collective-permute-done.69 = bf16[96,768]{1,0:T(8,128)(2,1)S(1)} collective-permute-done((bf16[96,768]{1,0:T(8,128)(2,1)S(1)}, bf16[96,768]{1,0:T(8,128)(2,1)S(1)}, u32[]{:S(2)}, u32[]{:S(2)}) %collective-permute-start.69) | collective-permute-done | bytes 147488 | tf_op jit(solution)/shard_map/ppermute | solution.py:220
  237.1 10.5 %attend_backward.2 = (bf16[512,256]{1,0:T(8,128)(2,1)S(1)}, f32[1,256]{1,0:T(1,128)S(1)}, bf16[512,384]{1,0:T(8,128)(2,1)S(1)}, bf16[512,384]{1,0:T(8,128)(2,1)S...) custom-call(s32[6]{0:T(128)S(1)} %squeeze.18.rng, ...), custom_call_target="tpu_custom_call" | custom-call | flops 9059696640 | bytes 3932160 | tf_op jit(solution)/shard_map/attend_backward/pallas_call | solution.py:437
  250.1 7.4 %attend_backward.3 = (bf16[512,256]{1,0:T(8,128)(2,1)S(1)}, f32[1,256]{1,0:T(1,128)S(1)}, bf16[512,384]{1,0:T(8,128)(2,1)S(1)}, bf16[512,384]{1,0:T(8,128)(2,1)S...) custom-call(s32[6]{0:T(128)S(1)} %squeeze.24.rng, ...), custom_call_target="tpu_custom_call" | custom-call | flops 9059696640 | bytes 3932160 | tf_op jit(solution)/shard_map/attend_backward/pallas_call | solution.py:437
  258.3 8.3 %collective-permute-start.29 = (bf16[512,384]{1,0:T(8,128)(2,1)S(1)}, bf16[512,384]{1,0:T(8,128)(2,1)S(1)}, u32[]{:S(2)}, u32[]{:S(2)}) collective-permute-start(bf16[512,384]{1,0:T(8,128)(2,1)S(1)} %get-tuple-element.38), channel_id=1, source_target_pairs={{0,4},{4,8},{8,12},{1,5},{5,9},{9,13},{2,6},{6,10},{10,14},{3,7},{... | collective-permute-start | bytes 1179656 | tf_op jit(solution)/shard_map/ppermute | solution.py:224
  276.8 5.0 %collective-permute-done.61 = bf16[192,384]{1,0:T(8,128)(2,1)S(1)} collective-permute-done((bf16[192,384]{1,0:T(8,128)(2,1)S(1)}, bf16[192,384]{1,0:T(8,128)(2,1)S(1)}, u32[]{:S(2)}, u32[]{:S(2)}) %collective-permute-start.61) | collective-permute-done | bytes 147488 | tf_op jit(solution)/shard_map/ppermute | solution.py:220
  297.9 3.7 collective-permute-done.63
  301.6 4.3 %collective-permute-start.40 = (bf16[512,384]{1,0:T(8,128)(2,1)S(1)}, bf16[512,384]{1,0:T(8,128)(2,1)S(1)}, u32[]{:S(2)}, u32[]{:S(2)}) collective-permute-start(bf16[512,384]{1,0:T(8,128)(2,1)S(1)} %get-tuple-element.45), channel_id=1, source_target_pairs={{0,4},{4,8},{8,12},{1,5},{5,9},{9,13},{2,6},{6,10},{10,14},{3,7},{... | collective-permute-start | bytes 1179656 | tf_op jit(solution)/shard_map/ppermute | solution.py:224
  311.6 4.1 %collective-permute-done.50 = bf16[96,192]{0,1:T(8,128)(2,1)S(1)} collective-permute-done((bf16[96,192]{0,1:T(8,128)(2,1)S(1)}, bf16[96,192]{0,1:T(8,128)(2,1)S(1)}, u32[]{:S(2)}, u32[]{:S(2)}) %collective-permute-start.50) | collective-permute-done | bytes 36896 | tf_op jit(solution)/shard_map/ppermute | solution.py:220
  316.6 4.0 collective-permute-done.64
  331.5 4.4 %collective-permute-start.41 = (bf16[512,384]{1,0:T(8,128)(2,1)S(1)}, bf16[512,384]{1,0:T(8,128)(2,1)S(1)}, u32[]{:S(2)}, u32[]{:S(2)}) collective-permute-start(bf16[512,384]{1,0:T(8,128)(2,1)S(1)} %add_convert_fusion.2), channel_id=1, source_target_pairs={{0,4},{4,8},{8,12},{1,5},{5,9},{9,13},{2,6},{6,10},{10,14},{3,7},{... | collective-permute-start | bytes 1179656 | tf_op jit(solution)/shard_map/ppermute | solution.py:224
  337.5 4.6 %collective-permute-start.30 = (bf16[512,384]{1,0:T(8,128)(2,1)S(1)}, bf16[512,384]{1,0:T(8,128)(2,1)S(1)}, u32[]{:S(2)}, u32[]{:S(2)}) collective-permute-start(bf16[512,384]{1,0:T(8,128)(2,1)S(1)} %add_convert_fusion.5), channel_id=1, source_target_pairs={{0,4},{4,8},{8,12},{1,5},{5,9},{9,13},{2,6},{6,10},{10,14},{3,7},{... | collective-permute-start | bytes 1179656 | tf_op jit(solution)/shard_map/ppermute | solution.py:224
  347.5 4.3 %collective-permute-done.32 = bf16[512,384]{1,0:T(8,128)(2,1)S(1)} collective-permute-done((bf16[512,384]{1,0:T(8,128)(2,1)S(1)}, bf16[512,384]{1,0:T(8,128)(2,1)S(1)}, u32[]{:S(2)}, u32[]{:S(2)}) %collective-permute-start.32) | collective-permute-done | bytes 393248 | tf_op jit(solution)/shard_map/ppermute | solution.py:224
  364.6 4.3 %collective-permute-done.60 = f32[3456]{0:T(1024)S(1)} collective-permute-done((f32[3456]{0:T(1024)S(1)}, f32[3456]{0:T(1024)S(1)}, u32[]{:S(2)}, u32[]{:S(2)}) %collective-permute-start.60) | collective-permute-done | bytes 13856 | tf_op jit(solution)/shard_map/ppermute | solution.py:220
  379.0 4.5 %collective-permute-done.54 = bf16[96,384]{1,0:T(8,128)(2,1)S(1)} collective-permute-done((bf16[96,384]{1,0:T(8,128)(2,1)S(1)}, bf16[96,384]{1,0:T(8,128)(2,1)S(1)}, u32[]{:S(2)}, u32[]{:S(2)}) %collective-permute-start.54) | collective-permute-done | bytes 73760 | tf_op jit(solution)/shard_map/ppermute | solution.py:220
  390.5 3.8 collective-permute-done.34
  (511 shorter events, 210.3 us)
Async XLA Ops:
  6.6 27.1 %collective-permute-start.6 = (bf16[208,384]{1,0:T(8,128)(2,1)}, bf16[208,384]{1,0:T(8,128)(2,1)}, u32[]{:S(2)}, u32[]{:S(2)}) collective-permute-start(bf16[208,384]{1,0:T(8,128)(2,1)} %pad_maximum_fusion.19), channel_id=1, source_target_pairs={{0,16},{16,0},{1,17},{17,1},{2,18},{18,2},{3,19},{19,3},{4,20},{20... | collective-permute-start | bytes 479240 | tf_op jit(solution)/shard_map/ppermute | solution.py:220
  10.8 38.0 %collective-permute-start = (bf16[384,256]{0,1:T(8,128)(2,1)S(1)}, bf16[384,256]{0,1:T(8,128)(2,1)}, u32[]{:S(2)}, u32[]{:S(2)}) collective-permute-start(bf16[384,256]{0,1:T(8,128)(2,1)S(1)} %pad.14), channel_id=1, source_target_pairs={{0,16},{16,0},{1,17},{17,1},{2,18},{18,2},{3,19},{19,3},{4,20},{20... | collective-permute-start | bytes 589832 | tf_op jit(solution)/shard_map/ppermute | solution.py:220
  25.7 17.2 %collective-permute-start.4 = (bf16[512,384]{1,0:T(8,128)(2,1)}, bf16[512,384]{1,0:T(8,128)(2,1)}, u32[]{:S(2)}, u32[]{:S(2)}) collective-permute-start(bf16[512,384]{1,0:T(8,128)(2,1)} %fusion.16.rest_2_), channel_id=1, source_target_pairs={{4,0},{8,4},{12,8},{5,1},{9,5},{13,9},{6,2},{10,6},{14,10},{7,3},{... | collective-permute-start | bytes 1179656 | tf_op jit(solution)/shard_map/ppermute | solution.py:224
  27.0 17.2 %collective-permute-start.2 = (bf16[512,384]{1,0:T(8,128)(2,1)}, bf16[512,384]{1,0:T(8,128)(2,1)}, u32[]{:S(2)}, u32[]{:S(2)}) collective-permute-start(bf16[512,384]{1,0:T(8,128)(2,1)} %fusion.16.rest_2_), channel_id=1, source_target_pairs={{0,4},{4,8},{8,12},{1,5},{5,9},{9,13},{2,6},{6,10},{10,14},{3,7},{... | collective-permute-start | bytes 1179656 | tf_op jit(solution)/shard_map/ppermute | solution.py:224
  37.0 14.6 %collective-permute-start.17 = (bf16[512,384]{1,0:T(8,128)(2,1)S(1)}, bf16[512,384]{1,0:T(8,128)(2,1)S(1)}, u32[]{:S(2)}, u32[]{:S(2)}) collective-permute-start(bf16[512,384]{1,0:T(8,128)(2,1)S(1)} %fusion.19.rest_2_), channel_id=1, source_target_pairs={{4,0},{8,4},{12,8},{5,1},{9,5},{13,9},{6,2},{10,6},{14,10},{7,3},{... | collective-permute-start | bytes 1179656 | tf_op jit(solution)/shard_map/ppermute | solution.py:224
  38.3 14.6 %collective-permute-start.15 = (bf16[512,384]{1,0:T(8,128)(2,1)S(1)}, bf16[512,384]{1,0:T(8,128)(2,1)S(1)}, u32[]{:S(2)}, u32[]{:S(2)}) collective-permute-start(bf16[512,384]{1,0:T(8,128)(2,1)S(1)} %fusion.19.rest_2_), channel_id=1, source_target_pairs={{0,4},{4,8},{8,12},{1,5},{5,9},{9,13},{2,6},{6,10},{10,14},{3,7},{... | collective-permute-start | bytes 1179656 | tf_op jit(solution)/shard_map/ppermute | solution.py:224
  42.9 16.4 %collective-permute-start.5 = (bf16[512,384]{1,0:T(8,128)(2,1)}, bf16[512,384]{1,0:T(8,128)(2,1)S(1)}, u32[]{:S(2)}, u32[]{:S(2)}) collective-permute-start(bf16[512,384]{1,0:T(8,128)(2,1)} %collective-permute-done.4.rest_3_), channel_id=1, source_target_pairs={{4,0},{8,4},{12,8},{5,1},{9,5},{13,9},{6,2},{10,6},{14,10},{7,3},{... | collective-permute-start | bytes 1179656 | tf_op jit(solution)/shard_map/ppermute | solution.py:224
  44.2 16.7 %collective-permute-start.3 = (bf16[512,384]{1,0:T(8,128)(2,1)}, bf16[512,384]{1,0:T(8,128)(2,1)S(1)}, u32[]{:S(2)}, u32[]{:S(2)}) collective-permute-start(bf16[512,384]{1,0:T(8,128)(2,1)} %collective-permute-done.2.rest_1_), channel_id=1, source_target_pairs={{0,4},{4,8},{8,12},{1,5},{5,9},{9,13},{2,6},{6,10},{10,14},{3,7},{... | collective-permute-start | bytes 1179656 | tf_op jit(solution)/shard_map/ppermute | solution.py:224
  51.6 17.1 %collective-permute-start.18 = (bf16[512,384]{1,0:T(8,128)(2,1)S(1)}, bf16[512,384]{1,0:T(8,128)(2,1)S(1)}, u32[]{:S(2)}, u32[]{:S(2)}) collective-permute-start(bf16[512,384]{1,0:T(8,128)(2,1)S(1)} %collective-permute-done.17.rest_3_), channel_id=1, source_target_pairs={{4,0},{8,4},{12,8},{5,1},{9,5},{13,9},{6,2},{10,6},{14,10},{7,3},{... | collective-permute-start | bytes 1179656 | tf_op jit(solution)/shard_map/ppermute | solution.py:224
  53.0 15.8 %collective-permute-start.16 = (bf16[512,384]{1,0:T(8,128)(2,1)S(1)}, bf16[512,384]{1,0:T(8,128)(2,1)S(1)}, u32[]{:S(2)}, u32[]{:S(2)}) collective-permute-start(bf16[512,384]{1,0:T(8,128)(2,1)S(1)} %collective-permute-done.15.rest_1_), channel_id=1, source_target_pairs={{0,4},{4,8},{8,12},{1,5},{5,9},{9,13},{2,6},{6,10},{10,14},{3,7},{... | collective-permute-start | bytes 1179656 | tf_op jit(solution)/shard_map/ppermute | solution.py:224
  77.7 17.6 %collective-permute-start.20 = (bf16[256,768]{1,0:T(8,128)(2,1)S(1)}, bf16[256,768]{1,0:T(8,128)(2,1)}, u32[]{:S(2)}, u32[]{:S(2)}) collective-permute-start(bf16[256,768]{1,0:T(8,128)(2,1)S(1)} %fusion.20), channel_id=1, source_target_pairs={{0,2},{1,3},{2,0},{3,1},{4,6},{5,7},{6,4},{7,5},{8,10},{9,11},{10,... | collective-permute-start | bytes 1179656 | tf_op jit(solution)/shard_map/ppermute | solution.py:220
  79.6 21.8 %collective-permute-start.10 = (bf16[384,768]{1,0:T(8,128)(2,1)}, bf16[384,768]{1,0:T(8,128)(2,1)}, u32[]{:S(2)}, u32[]{:S(2)}) collective-permute-start(bf16[384,768]{1,0:T(8,128)(2,1)} %convert_element_type.439), channel_id=1, source_target_pairs={{0,16},{16,0},{1,17},{17,1},{2,18},{18,2},{3,19},{19,3},{4,20},{20... | collective-permute-start | bytes 1769480 | tf_op jit(solution)/shard_map/ppermute | solution.py:220
  98.4 16.4 %collective-permute-start.11 = (bf16[768,384]{1,0:T(8,128)(2,1)S(1)}, bf16[768,384]{1,0:T(8,128)(2,1)S(1)}, u32[]{:S(2)}, u32[]{:S(2)}) collective-permute-start(bf16[768,384]{1,0:T(8,128)(2,1)S(1)} %convert_element_type.441), channel_id=1, source_target_pairs={{0,16},{16,0},{1,17},{17,1},{2,18},{18,2},{3,19},{19,3},{4,20},{20... | collective-permute-start | bytes 1769480 | tf_op jit(solution)/shard_map/ppermute | solution.py:220
  124.8 17.4 %collective-permute-start.13 = (bf16[256,768]{1,0:T(8,128)(2,1)}, bf16[256,768]{1,0:T(8,128)(2,1)}, u32[]{:S(2)}, u32[]{:S(2)}) collective-permute-start(bf16[256,768]{1,0:T(8,128)(2,1)} %fusion.18), channel_id=1, source_target_pairs={{0,2},{1,3},{2,0},{3,1},{4,6},{5,7},{6,4},{7,5},{8,10},{9,11},{10,... | collective-permute-start | bytes 1179656 | tf_op jit(solution)/shard_map/ppermute | solution.py:220
  159.8 16.3 %collective-permute-start.66 = (bf16[384,768]{1,0:T(8,128)(2,1)S(1)}, bf16[384,768]{1,0:T(8,128)(2,1)S(1)}, u32[]{:S(2)}, u32[]{:S(2)}) collective-permute-start(bf16[384,768]{1,0:T(8,128)(2,1)S(1)} %fusion.12), channel_id=1, source_target_pairs={{0,16},{16,0},{1,17},{17,1},{2,18},{18,2},{3,19},{19,3},{4,20},{20... | collective-permute-start | bytes 1769480 | tf_op jit(solution)/shard_map/ppermute | solution.py:220
  162.9 25.3 %collective-permute-start.71 = (bf16[768,384]{1,0:T(8,128)(2,1)S(1)}, bf16[768,384]{1,0:T(8,128)(2,1)S(1)}, u32[]{:S(2)}, u32[]{:S(2)}) collective-permute-start(bf16[768,384]{1,0:T(8,128)(2,1)S(1)} %fusion.13), channel_id=1, source_target_pairs={{0,16},{16,0},{1,17},{17,1},{2,18},{18,2},{3,19},{19,3},{4,20},{20... | collective-permute-start | bytes 1769480 | tf_op jit(solution)/shard_map/ppermute | solution.py:220
  168.3 21.5 %collective-permute-start.27 = (bf16[256,768]{1,0:T(8,128)(2,1)S(1)}, bf16[256,768]{1,0:T(8,128)(2,1)S(1)}, u32[]{:S(2)}, u32[]{:S(2)}) collective-permute-start(bf16[256,768]{1,0:T(8,128)(2,1)S(1)} %fusion.22), channel_id=1, source_target_pairs={{0,2},{1,3},{2,0},{3,1},{4,6},{5,7},{6,4},{7,5},{8,10},{9,11},{10,... | collective-permute-start | bytes 1179656 | tf_op jit(solution)/shard_map/ppermute | solution.py:220
  171.6 19.9 %collective-permute-start.38 = (bf16[256,768]{1,0:T(8,128)(2,1)S(1)}, bf16[256,768]{1,0:T(8,128)(2,1)S(1)}, u32[]{:S(2)}, u32[]{:S(2)}) collective-permute-start(bf16[256,768]{1,0:T(8,128)(2,1)S(1)} %fusion.25), channel_id=1, source_target_pairs={{0,2},{1,3},{2,0},{3,1},{4,6},{5,7},{6,4},{7,5},{8,10},{9,11},{10,... | collective-permute-start | bytes 1179656 | tf_op jit(solution)/shard_map/ppermute | solution.py:220
  176.7 27.7 %collective-permute-start.67 = (bf16[192,768]{1,0:T(8,128)(2,1)S(1)}, bf16[192,768]{1,0:T(8,128)(2,1)}, u32[]{:S(2)}, u32[]{:S(2)}) collective-permute-start(bf16[192,768]{1,0:T(8,128)(2,1)S(1)} %dynamic-slice_convert_fusion.1), channel_id=1, source_target_pairs={{0,4},{4,0},{8,12},{12,8},{1,5},{5,1},{9,13},{13,9},{2,6},{6,2},{1... | collective-permute-start | bytes 884744 | tf_op jit(solution)/shard_map/ppermute | solution.py:220
  196.0 16.5 %collective-permute-start.72 = (bf16[384,384]{1,0:T(8,128)(2,1)S(1)}, bf16[384,384]{1,0:T(8,128)(2,1)S(1)}, u32[]{:S(2)}, u32[]{:S(2)}) collective-permute-start(bf16[384,384]{1,0:T(8,128)(2,1)S(1)} %dynamic-slice_convert_fusion), channel_id=1, source_target_pairs={{0,4},{4,0},{8,12},{12,8},{1,5},{5,1},{9,13},{13,9},{2,6},{6,2},{1... | collective-permute-start | bytes 884744 | tf_op jit(solution)/shard_map/ppermute | solution.py:220
  203.8 31.9 %collective-permute-start.28 = (bf16[256,768]{1,0:T(8,128)(2,1)}, bf16[256,768]{1,0:T(8,128)(2,1)S(1)}, u32[]{:S(2)}, u32[]{:S(2)}) collective-permute-start(bf16[256,768]{1,0:T(8,128)(2,1)} %convert_element_type.476), channel_id=1, source_target_pairs={{0,1},{1,0},{2,3},{3,2},{4,5},{5,4},{6,7},{7,6},{8,9},{9,8},{10,11... | collective-permute-start | bytes 1179656 | tf_op jit(solution)/shard_map/ppermute | solution.py:220
  203.9 44.4 %collective-permute-start.39 = (bf16[256,768]{1,0:T(8,128)(2,1)}, bf16[256,768]{1,0:T(8,128)(2,1)}, u32[]{:S(2)}, u32[]{:S(2)}) collective-permute-start(bf16[256,768]{1,0:T(8,128)(2,1)} %convert_element_type.505), channel_id=1, source_target_pairs={{0,1},{1,0},{2,3},{3,2},{4,5},{5,4},{6,7},{7,6},{8,9},{9,8},{10,11... | collective-permute-start | bytes 1179656 | tf_op jit(solution)/shard_map/ppermute | solution.py:220
  205.4 15.2 %collective-permute-start.68 = (bf16[96,768]{1,0:T(8,128)(2,1)S(1)}, bf16[96,768]{1,0:T(8,128)(2,1)S(1)}, u32[]{:S(2)}, u32[]{:S(2)}) collective-permute-start(bf16[96,768]{1,0:T(8,128)(2,1)S(1)} %dynamic-slice_convert_fusion.3), channel_id=1, source_target_pairs={{0,8},{4,12},{8,0},{12,4},{1,9},{5,13},{9,1},{13,5},{2,10},{6,14},... | collective-permute-start | bytes 442376 | tf_op jit(solution)/shard_map/ppermute | solution.py:220
  231.3 74.7 %collective-permute-start.70 = (bf16[192,768]{1,0:T(8,128)(2,1)S(1)}, bf16[192,768]{1,0:T(8,128)(2,1)S(1)}, u32[]{:S(2)}, u32[]{:S(2)}) collective-permute-start(bf16[192,768]{1,0:T(8,128)(2,1)S(1)} %maximum_select_fusion.13), channel_id=1, source_target_pairs={{0,4},{4,0},{8,12},{12,8},{1,5},{5,1},{9,13},{13,9},{2,6},{6,2},{1... | collective-permute-start | bytes 884744 | tf_op jit(solution)/shard_map/ppermute | solution.py:220
  233.2 75.2 %collective-permute-start.75 = (bf16[384,384]{1,0:T(8,128)(2,1)S(1)}, bf16[384,384]{1,0:T(8,128)(2,1)S(1)}, u32[]{:S(2)}, u32[]{:S(2)}) collective-permute-start(bf16[384,384]{1,0:T(8,128)(2,1)S(1)} %maximum_select_fusion.14), channel_id=1, source_target_pairs={{0,4},{4,0},{8,12},{12,8},{1,5},{5,1},{9,13},{13,9},{2,6},{6,2},{1... | collective-permute-start | bytes 884744 | tf_op jit(solution)/shard_map/ppermute | solution.py:220
  258.3 79.1 %collective-permute-start.29 = (bf16[512,384]{1,0:T(8,128)(2,1)S(1)}, bf16[512,384]{1,0:T(8,128)(2,1)S(1)}, u32[]{:S(2)}, u32[]{:S(2)}) collective-permute-start(bf16[512,384]{1,0:T(8,128)(2,1)S(1)} %get-tuple-element.38), channel_id=1, source_target_pairs={{0,4},{4,8},{8,12},{1,5},{5,9},{9,13},{2,6},{6,10},{10,14},{3,7},{... | collective-permute-start | bytes 1179656 | tf_op jit(solution)/shard_map/ppermute | solution.py:224
  266.5 75.5 %collective-permute-start.31 = (bf16[512,384]{1,0:T(8,128)(2,1)S(1)}, bf16[512,384]{1,0:T(8,128)(2,1)S(1)}, u32[]{:S(2)}, u32[]{:S(2)}) collective-permute-start(bf16[512,384]{1,0:T(8,128)(2,1)S(1)} %get-tuple-element.40), channel_id=1, source_target_pairs={{4,0},{8,4},{12,8},{5,1},{9,5},{13,9},{6,2},{10,6},{14,10},{7,3},{... | collective-permute-start | bytes 1179656 | tf_op jit(solution)/shard_map/ppermute | solution.py:224
  301.6 29.8 %collective-permute-start.40 = (bf16[512,384]{1,0:T(8,128)(2,1)S(1)}, bf16[512,384]{1,0:T(8,128)(2,1)S(1)}, u32[]{:S(2)}, u32[]{:S(2)}) collective-permute-start(bf16[512,384]{1,0:T(8,128)(2,1)S(1)} %get-tuple-element.45), channel_id=1, source_target_pairs={{0,4},{4,8},{8,12},{1,5},{5,9},{9,13},{2,6},{6,10},{10,14},{3,7},{... | collective-permute-start | bytes 1179656 | tf_op jit(solution)/shard_map/ppermute | solution.py:224
  306.0 30.0 %collective-permute-start.42 = (bf16[512,384]{1,0:T(8,128)(2,1)S(1)}, bf16[512,384]{1,0:T(8,128)(2,1)S(1)}, u32[]{:S(2)}, u32[]{:S(2)}) collective-permute-start(bf16[512,384]{1,0:T(8,128)(2,1)S(1)} %get-tuple-element.47), channel_id=1, source_target_pairs={{4,0},{8,4},{12,8},{5,1},{9,5},{13,9},{6,2},{10,6},{14,10},{7,3},{... | collective-permute-start | bytes 1179656 | tf_op jit(solution)/shard_map/ppermute | solution.py:224
  353.6 15.3 %collective-permute-start.52 = (bf16[384,384]{1,0:T(8,128)(2,1)S(1)}, bf16[384,384]{1,0:T(8,128)(2,1)S(1)}, u32[]{:S(2)}, u32[]{:S(2)}) collective-permute-start(bf16[384,384]{1,0:T(8,128)(2,1)S(1)} %fusion.29), channel_id=1, source_target_pairs={{0,16},{16,0},{1,17},{17,1},{2,18},{18,2},{3,19},{19,3},{4,20},{20... | collective-permute-start | bytes 884744 | tf_op jit(solution)/shard_map/ppermute | solution.py:220
  357.5 18.9 %collective-permute-start.44 = (bf16[256,768]{1,0:T(8,128)(2,1)}, bf16[256,768]{1,0:T(8,128)(2,1)}, u32[]{:S(2)}, u32[]{:S(2)}) collective-permute-start(bf16[256,768]{1,0:T(8,128)(2,1)} %fusion.27), channel_id=1, source_target_pairs={{0,1},{1,0},{2,3},{3,2},{4,5},{5,4},{6,7},{7,6},{8,9},{9,8},{10,11... | collective-permute-start | bytes 1179656 | tf_op jit(solution)/shard_map/ppermute | solution.py:220
  359.9 23.7 %collective-permute-start.33 = (bf16[256,768]{1,0:T(8,128)(2,1)}, bf16[256,768]{1,0:T(8,128)(2,1)}, u32[]{:S(2)}, u32[]{:S(2)}) collective-permute-start(bf16[256,768]{1,0:T(8,128)(2,1)} %fusion.24), channel_id=1, source_target_pairs={{0,1},{1,0},{2,3},{3,2},{4,5},{5,4},{6,7},{7,6},{8,9},{9,8},{10,11... | collective-permute-start | bytes 1179656 | tf_op jit(solution)/shard_map/ppermute | solution.py:220
  (118 other events, 989.7 us)

commit v2 on v1

--- a/solution.py
+++ b/solution.py
@@ -45,9 +45,9 @@
     return jnp.concatenate(parts, 0)
 
 
-def load_blocks(kv_refs, kvb, sem, tok):
+def load_blocks(kv_refs, kvb, sem, tok, slot_of):
     copies = [
-        pltpu.make_async_copy(ref, kvb.at[pl.ds(i * tok, tok)], sem.at[i])
+        pltpu.make_async_copy(ref, kvb.at[pl.ds(pl.multiple_of(slot_of(i) * tok, tok), tok)], sem.at[i])
         for i, ref in enumerate(kv_refs)
     ]
     for copy in copies:
@@ -61,7 +61,8 @@
     o_ref, lse_ref, kvb, st, acc, sem = rest[slots:]
     tok = q_ref.shape[0]
     wide = q_ref.shape[1]
-    load_blocks(kv_refs, kvb, sem, tok)
+    table = 3 * (tok // tq)
+    load_blocks(kv_refs, kvb, sem, tok, lambda i: rng[table + i])
     vfirst = 2 * heads * HEAD_DIM - wide
     voff = wide - heads * HEAD_DIM
     for t in range(tok // tq):
@@ -106,7 +107,8 @@
     kvb, dkv, dqt, sem = rest[2 * slots + 2 :]
     tok = q_ref.shape[0]
     wide = q_ref.shape[1]
-    load_blocks(kv_refs, kvb, sem, tok)
+    table = 3 * (tok // tq)
+    load_blocks(kv_refs, kvb, sem, tok, lambda i: rng[table + i])
     vfirst = 2 * heads * HEAD_DIM - wide
     voff = wide - heads * HEAD_DIM
     dkv[...] = jnp.zeros_like(dkv)
@@ -156,7 +158,7 @@
         dq_ref[pl.ds(qs, tq), :] = dq.astype(BF)
     bias_ref[...] = bias
     for i, ref in enumerate(dkv_refs):
-        ref[...] = dkv[i * tok : (i + 1) * tok, :].astype(BF)
+        ref[...] = dkv[pl.ds(pl.multiple_of(rng[table + i] * tok, tok), tok), :].astype(BF)
 
 
 def make_attention(slots, heads, tok, wide, packed):
@@ -213,30 +215,43 @@
     return forward, backward
 
 
+def after(value, *others):
+    return lax.optimization_barrier((value,) + others)[0]
+
+
 def make_body(n_shard, n_ctx, n_tp):
     bits = [1 << i for i in range(n_tp.bit_length() - 1)]
+    ctx_steps = [1 << i for i in range(n_ctx.bit_length() - 1)]
+    ctx_whole = not n_ctx & (n_ctx - 1)
 
     def exchange(value, axis, size, bit):
-        return lax.ppermute(value, axis, [(i, i ^ bit) for i in range(size)])
-
-    def shift(value, step):
-        pairs = [(i, i + step) for i in range(n_ctx) if 0 <= i + step < n_ctx]
+        return lax.ppermute(value, axis, [(i, i ^ bit) for i in range(size) if i ^ bit < size])
+
+    def even_swap(value):
+        return exchange(value, "ctx", n_ctx, 1)
+
+    def odd_swap(value):
+        pairs = []
+        for i in range(1, n_ctx - 1, 2):
+            pairs += [(i, i + 1), (i + 1, i)]
         return lax.ppermute(value, "ctx", pairs)
 
+    def swap(value, kind):
+        return odd_swap(value) if kind else even_swap(value)
+
     def ctx_sum(value):
-        if n_ctx & (n_ctx - 1):
+        if not ctx_whole:
             return lax.psum(value, "ctx")
         ci = lax.axis_index("ctx")
-        steps = [1 << i for i in range(n_ctx.bit_length() - 1)]
         cur = value
-        for bit in steps:
+        for bit in ctx_steps:
             half = cur.shape[0] // 2
             up = (ci // bit) % 2
             send = lax.dynamic_slice_in_dim(cur, (1 - up) * half, half, 0).astype(BF)
             keep = lax.dynamic_slice_in_dim(cur, up * half, half, 0)
             cur = keep + exchange(send, "ctx", n_ctx, bit).astype(F32)
         cur = cur.astype(BF)
-        for bit in reversed(steps):
+        for bit in reversed(ctx_steps):
             other = exchange(cur, "ctx", n_ctx, bit)
             up = (ci // bit) % 2
             cur = jnp.where(
@@ -270,6 +285,7 @@
         pad = wide - cols
         packed = 2 * cols
         half = tok // 2
+        every = range(rows)
         si = lax.axis_index("shard")
         ci = lax.axis_index("ctx")
         core = lax.axis_index("tp") % 2
@@ -294,11 +310,18 @@
                 return jnp.concatenate([own, exchange(own, "shard", 2, 1)], axis)
             return rolled(lax.all_gather(own, "shard", axis=axis, tiled=True), axis)
 
-        def shard_sum(make, axis):
+        def gathered_in_order(own):
             if n_shard == 2:
-                send = make(part, width).astype(BF)
-                return make(0, part) + exchange(send, "shard", 2, 1).astype(F32)
-            whole = unrolled(make(0, width), axis)
+                other = exchange(own, "shard", 2, 1)
+                return jnp.where(
+                    si == 0, jnp.concatenate([own, other], 0), jnp.concatenate([other, own], 0)
+                )
+            return lax.all_gather(own, "shard", axis=0, tiled=True)
+
+        def shard_sum(own, send, axis):
+            if n_shard == 2:
+                return own + exchange(send.astype(BF), "shard", 2, 1).astype(F32)
+            whole = unrolled(jnp.concatenate([own, send], axis), axis)
             return lax.psum_scatter(whole, "shard", scatter_dimension=axis, tiled=True)
 
         def own_half(value):
@@ -307,8 +330,11 @@
         def other_half(value):
             return lax.dynamic_slice_in_dim(value, (1 - core) * half, half, 0)
 
-        def tp_sum(own, send):
+        def core_sum(own, send):
             total = own + exchange(send.astype(BF), "tp", n_tp, 1).astype(F32)
+            return total.astype(BF) if len(bits) > 1 else total
+
+        def chip_sum(total):
             for bit in bits[1:]:
                 total = total.astype(BF)
                 total = total.astype(F32) + exchange(total, "tp", n_tp, bit).astype(F32)
@@ -321,27 +347,14 @@
             first, second = pair[:half], pair[half:]
             return jnp.where(core == 0, pair, jnp.concatenate([second, first], 0))
 
-        qkv_low = qkv_weight.astype(BF)
-        kv_own = qkv_low[:, 1:].reshape(part, packed)
-        q_own = jnp.pad(qkv_low[:, 0], ((0, 0), (0, pad)))
-        w_kv = gathered(kv_own, 0)
-        w_q = gathered(q_own, 0)
-        vec_own = jnp.stack(
-            [out_bias, first_gain, first_shift, outer_bias, second_gain, second_shift]
-        ).astype(BF)
-        vec_own = jnp.pad(vec_own, ((0, 10), (0, 0)))
-        wo_vec = gathered(jnp.concatenate([out_weight.astype(BF), vec_own], 0), 1)
-        w_out = jnp.concatenate([jnp.zeros((pad, width), BF), wo_vec[:cols]], 0)
-        vectors = wo_vec[cols : cols + 6].astype(F32)
-        w_in = gathered(inner_weight.astype(BF), 0)
-        w_outer = gathered(outer_weight.astype(BF), 1)
-
-        x = rolled(hidden_in, 2)
-        cot = rolled(cotangent, 2)
+        kv_own = qkv_weight[:, 1:].astype(BF).reshape(part, packed)
+        w_kv = gathered_in_order(kv_own)
+        q_own = jnp.pad(after(qkv_weight, kv_own)[:, 0].astype(BF), ((0, 0), (0, pad)))
+        w_q = gathered_in_order(q_own)
 
         before = jnp.full((rows, reach * tok), -1, jnp.int32)
-        after = jnp.full((rows, reach * tok), 1 << 20, jnp.int32)
-        padded = jnp.concatenate([before, segment_ids, after], 1)
+        behind = jnp.full((rows, reach * tok), 1 << 20, jnp.int32)
+        padded = jnp.concatenate([before, segment_ids, behind], 1)
         key_seg = lax.dynamic_slice_in_dim(padded, ci * tok, slots * tok, 1)
         q_seg = lax.dynamic_slice_in_dim(segment_ids, ci * tok, tok, 1)
         q_seg = q_seg.reshape(rows, 2, half)
@@ -350,24 +363,47 @@
         high = (jnp.sum(key_seg[:, None, :] <= q_seg[:, :, -1:], -1) + half - 1) // half
         begin = jnp.broadcast_to(jnp.stack([core * half, (1 - core) * half])[None], (rows, 2))
         ranges = jnp.stack([low, high, begin], -1).reshape(rows, 6).astype(jnp.int32)
+        side = 1 - 2 * (ci % 2)
+        places = [jnp.int32(reach) + 0 * side]
+        for d in range(1, reach + 1):
+            places += [reach + d * side, reach - d * side]
+        places = jnp.broadcast_to(jnp.stack(places)[None], (rows, slots))
+        ranges = jnp.concatenate([ranges, places.astype(jnp.int32)], 1)
         q_seg3 = jnp.tile(q_seg[:, :, None, :], (1, 1, 1, heads))
         key_col = key_seg[:, :, None]
 
         v_bias = jnp.concatenate([jnp.zeros((cols,), F32), qv_bias[1]])
         q_bias = jnp.pad(qv_bias[0], (0, pad))
 
-        def blocks_of(own):
-            left, right = [own], [own]
-            for _ in range(reach):
-                left.append(shift(left[-1], 1))
-                right.append(shift(right[-1], -1))
-            return left[:0:-1] + [own] + right[1:]
-
-        kv = [blocks_of((dot(x[r], w_kv) + v_bias).astype(BF)) for r in range(rows)]
+        kv = []
+        for r in every:
+            own = (dot(hidden_in[r], w_kv) + v_bias).astype(BF)
+            if r:
+                own = after(own, *kv[-1][1:3])
+            found = [own]
+            last = [own, own]
+            for d in range(1, reach + 1):
+                even, odd = even_swap(last[1]), odd_swap(last[0])
+                found += [even, odd]
+                last = [even, odd]
+            kv.append(found)
         q = [
-            ((dot(x[r], w_q) + q_bias).astype(BF) * jnp.asarray(HEAD_DIM**-0.5, BF))
-            for r in range(rows)
+            ((dot(hidden_in[r], w_q) + q_bias).astype(BF) * jnp.asarray(HEAD_DIM**-0.5, BF))
+            for r in every
         ]
+
+        late = kv[0][0]
+        vec_own = jnp.concatenate(
+            [out_bias, first_gain, first_shift, outer_bias, second_gain, second_shift]
+        )
+        vec_own = jnp.pad(vec_own.reshape(6, part), ((0, 10), (0, 0)))
+        wo_own = jnp.concatenate([after(out_weight, late), vec_own], 0).astype(BF)
+        wo_vec = gathered(wo_own, 1)
+        w_out = jnp.concatenate([jnp.zeros((pad, width), BF), wo_vec[:cols]], 0)
+        vectors = wo_vec[cols : cols + 6].astype(F32)
+        w_in = gathered(after(inner_weight, wo_own).astype(BF), 0)
+        w_outer = gathered(after(outer_weight, wo_own).astype(BF), 1)
+        bo, g1, s1, bd, g2, s2 = [vectors[i] for i in range(6)]
 
         def normed(summed):
             average = jnp.mean(summed, -1, keepdims=True)
@@ -384,127 +420,182 @@
                 - hat * jnp.mean(inner * hat, -1, keepdims=True)
             )
 
-        bo, g1, s1, bd, g2, s2 = [vectors[i] for i in range(6)]
-        saved = []
-        for r in range(rows):
-            o, lse = attend_fwd(ranges[r], q[r], q_seg3[r], key_col[r], *kv[r])
-            total = tp_sum(dot(o[:half], w_out), dot(o[half:], w_out))
-            h1 = own_half(x[r]).astype(F32) + total + bo
-            hat1, scale1 = normed(h1)
-            y1 = hat1 * g1 + s1
-            y1b = both_halves(y1.astype(BF))
-            a = dot(y1b, w_in) + inner_bias
+        x_res = [rolled(own_half(hidden_in[r]), 1).astype(F32) for r in every]
+        cots = [rolled(own_half(cotangent[r]), 1).astype(F32) for r in every]
+
+        def chain(steps, first_gate=None):
+            gate = first_gate
+            for r in every:
+                gate = steps(r, gate)
+            return gate
+
+        def gated(value, gate):
+            return value if gate is None else after(value, gate)
+
+        o, lse, sent1 = [None] * rows, [None] * rows, [None] * rows
+
+        def stage1(r, gate):
+            o[r], lse[r] = attend_fwd(ranges[r], gated(q[r], gate), q_seg3[r], key_col[r], *kv[r])
+            send = dot(o[r][half:], w_out)
+            sent1[r] = core_sum(dot(o[r][:half], w_out), send)
+            return sent1[r]
+
+        gate = chain(stage1)
+
+        hat1, scale1, y1, y1b = [None] * rows, [None] * rows, [None] * rows, [None] * rows
+        u, slope, sent2 = [None] * rows, [None] * rows, [None] * rows
+
+        def stage2(r, gate):
+            total = gated(chip_sum(sent1[r]), gate)
+            hat1[r], scale1[r] = normed(x_res[r] + total + bo)
+            y1[r] = hat1[r] * g1 + s1
+            y1b[r] = both_halves(y1[r].astype(BF))
+            a = dot(y1b[r], w_in) + inner_bias
             cdf = 0.5 * (1.0 + lax.erf(a * (0.5**0.5)))
-            u = (a * cdf).astype(BF)
-            slope = (cdf + a * jnp.exp(-0.5 * a * a) * 0.3989422804014327).astype(BF)
-            total = tp_sum(dot(u[:half], w_outer), dot(u[half:], w_outer))
-            h2 = y1 + total + bd
-            hat2, scale2 = normed(h2)
-            saved.append((o, lse, hat1, scale1, y1b, u, slope, hat2, scale2))
-
-        outputs = []
-        d_vec = jnp.zeros((6, width), F32)
-        d_bi = jnp.zeros((units,), F32)
-        d_bq = jnp.zeros((wide,), F32)
-        d_bv = jnp.zeros((cols,), F32)
-        d2b, d1b, dab, dqs, dkvs, dh1s = [], [], [], [], [], []
-        for r in range(rows):
-            o, lse, hat1, scale1, y1b, u, slope, hat2, scale2 = saved[r]
-            c = own_half(cot[r]).astype(F32)
-            result = (hat2 * g2 + s2).astype(BF)
-            outputs.append(in_order(both_halves(unrolled(result, 1))))
-            dh2 = norm_back(c, g2, hat2, scale2)
-            dh2b = both_halves(dh2.astype(BF))
-            du = dot_nt(dh2b, w_outer)
-            da = du * slope.astype(F32)
-            d_bi = d_bi + jnp.sum(da, 0)
-            da_low = da.astype(BF)
-            total = tp_sum(dot_nt(da_low[:half], w_in), dot_nt(da_low[half:], w_in))
-            dy1 = dh2 + total
-            dh1 = norm_back(dy1, g1, hat1, scale1)
-            dh1b = both_halves(dh1.astype(BF))
-            d_vec = d_vec + jnp.stack(
-                [
-                    jnp.sum(dh1, 0),
-                    jnp.sum(dy1 * hat1, 0),
-                    jnp.sum(dy1, 0),
-                    jnp.sum(dh2, 0),
-                    jnp.sum(c * hat2, 0),
-                    jnp.sum(c, 0),
-                ]
-            )
-            do = dot_nt(dh1b, w_out).astype(BF)
-            res = attend_bwd(ranges[r], q[r], q_seg3[r], key_col[r], o, do, lse, *kv[r])
-            dq, bias = res[:2]
-            parts = res[2:]
-            d_bq = d_bq + bias[0]
-            carry_right = carry_left = None
+            u[r] = (a * cdf).astype(BF)
+            slope[r] = (cdf + a * jnp.exp(-0.5 * a * a) * 0.3989422804014327).astype(BF)
+            send = dot(u[r][half:], w_outer)
+            sent2[r] = core_sum(dot(u[r][:half], w_outer), send)
+            return sent2[r]
+
+        gate = chain(stage2, gate)
+
+        result, dh2, d2b, dab, sent3 = ([None] * rows for _ in range(5))
+        d_vec2, d_bi = [None] * rows, [None] * rows
+
+        def stage3(r, gate):
+            total = gated(chip_sum(sent2[r]), gate)
+            hat2, scale2 = normed(y1[r] + total + bd)
+            c = cots[r]
+            result[r] = (hat2 * g2 + s2).astype(BF)
+            dh2[r] = norm_back(c, g2, hat2, scale2)
+            d2b[r] = both_halves(dh2[r].astype(BF))
+            d_vec2[r] = [jnp.sum(dh2[r], 0), jnp.sum(c * hat2, 0), jnp.sum(c, 0)]
+            da = dot_nt(d2b[r], w_outer) * slope[r].astype(F32)
+            d_bi[r] = jnp.sum(da, 0)
+            dab[r] = da.astype(BF)
+            send = dot_nt(dab[r][half:], w_in)
+            sent3[r] = core_sum(dot_nt(dab[r][:half], w_in), send)
+            return sent3[r]
+
+        gate = chain(stage3, gate)
+
+        def over_rows(terms):
+            return functools.reduce(lambda p, q: p + q, terms)
+
+        send_outer = over_rows(dot_tn(gated(u[r], gate), d2b[r][:, part:]) for r in every).astype(BF)
+        send_in = over_rows(dot_tn(y1b[r][:, part:], gated(dab[r], gate)) for r in every).astype(BF)
+        gate = send_in
+
+        dh1, d1b, d_vec1, dqs, biases, parts = ([None] * rows for _ in range(6))
+
+        def stage4(r, gate):
+            total = gated(chip_sum(sent3[r]), gate)
+            dy1 = dh2[r] + total
+            dh1[r] = norm_back(dy1, g1, hat1[r], scale1[r])
+            d1b[r] = both_halves(dh1[r].astype(BF))
+            d_vec1[r] = [jnp.sum(dh1[r], 0), jnp.sum(dy1 * hat1[r], 0), jnp.sum(dy1, 0)]
+            do = dot_nt(d1b[r], w_out).astype(BF)
+            res = attend_bwd(ranges[r], q[r], q_seg3[r], key_col[r], o[r], do, lse[r], *kv[r])
+            dqs[r], biases[r], parts[r] = res[0], res[1][0], res[2:]
+            return res[0]
+
+        gate = chain(stage4, gate)
+
+        own_outer = over_rows(dot_tn(u[r], d2b[r][:, :part]) for r in every)
+        own_in = over_rows(dot_tn(y1b[r][:, :part], dab[r]) for r in every)
+        g_outer = shard_sum(own_outer, send_outer, 1)
+        g_in = shard_sum(own_in, send_in, 0)
+
+        dkvs, d_bv = [None] * rows, [None] * rows
+        for r in every:
+            carry = [None, None]
             for d in range(reach, 0, -1):
-                right, left = parts[reach + d], parts[reach - d]
-                if carry_right is not None:
-                    right = (right.astype(F32) + carry_right.astype(F32)).astype(BF)
-                    left = (left.astype(F32) + carry_left.astype(F32)).astype(BF)
-                carry_right, carry_left = shift(right, 1), shift(left, -1)
-            dkv = parts[reach].astype(F32)
-            if carry_right is not None:
-                dkv = dkv + carry_right.astype(F32) + carry_left.astype(F32)
-            d_bv = d_bv + jnp.sum(dkv[:, cols:], 0)
-            d2b.append(dh2b)
-            d1b.append(dh1b)
-            dab.append(da_low)
-            dqs.append(dq)
-            dkvs.append(dkv.astype(BF))
-            dh1s.append(dh1)
-
-        hidden_grads = []
-        for r in range(rows):
-            total = tp_sum(
-                dot_nt(own_half(dqs[r]), w_q) + dot_nt(own_half(dkvs[r]), w_kv),
-                dot_nt(other_half(dqs[r]), w_q) + dot_nt(other_half(dkvs[r]), w_kv),
-            )
-            grad = unrolled((dh1s[r] + total).astype(BF), 1)
-            hidden_grads.append(in_order(both_halves(grad)))
-
-        every = range(rows)
-
-        def total_of(terms):
-            return functools.reduce(lambda p, q: p + q, terms)
-
-        g_outer = shard_sum(lambda a, b: total_of(dot_tn(saved[r][5], d2b[r][:, a:b]) for r in every), 1)
-        g_in = shard_sum(lambda a, b: total_of(dot_tn(saved[r][4][:, a:b], dab[r]) for r in every), 0)
-        g_out = shard_sum(
-            lambda a, b: total_of(dot_tn(saved[r][0], d1b[r][:, a:b]) for r in every)[pad:], 1
+                pair = [parts[r][2 * d - 1], parts[r][2 * d]]
+                if carry[0] is not None:
+                    pair = [
+                        (p.astype(F32) + c.astype(F32)).astype(BF) for p, c in zip(pair, carry)
+                    ]
+                even, odd = even_swap(pair[0]), odd_swap(pair[1])
+                carry = [odd, even]
+            total = parts[r][0].astype(F32)
+            if carry[0] is not None:
+                total = total + carry[0].astype(F32) + carry[1].astype(F32)
+            d_bv[r] = jnp.sum(total[:, cols:], 0)
+            dkvs[r] = total.astype(BF)
+
+        if n_shard == 2:
+            x_own = [jnp.where(si == 0, hidden_in[r][:, :part], hidden_in[r][:, part:]) for r in every]
+            x_send = [jnp.where(si == 0, hidden_in[r][:, part:], hidden_in[r][:, :part]) for r in every]
+        else:
+            x_all = [rolled(hidden_in[r], 1) for r in every]
+            x_own = [x_all[r][:, :part] for r in every]
+            x_send = [x_all[r][:, part:] for r in every]
+        send_mix = jnp.concatenate(
+            [
+                over_rows(dot_tn(o[r], d1b[r][:, part:]) for r in every)[pad:].astype(BF),
+                over_rows(dot_tn(dqs[r], x_send[r]) for r in every)[:cols].astype(BF),
+            ],
+            0,
         )
-        g_q = shard_sum(lambda a, b: total_of(dot_tn(x[r][:, a:b], dqs[r]) for r in every)[:, :cols], 0)
-        g_kv = shard_sum(lambda a, b: total_of(dot_tn(x[r][:, a:b], dkvs[r]) for r in every), 0)
-        g_outer = ctx_sum(g_outer)
-        g_in = ctx_sum(g_in)
-        g_out = ctx_sum(g_out)
-        g_q = ctx_sum(g_q)
-        g_kv = ctx_sum(g_kv)
-        grad_qkv = jnp.concatenate([g_q[:, None], g_kv.reshape(part, 2, cols)], 1)
-
+        own_mix = jnp.concatenate(
+            [
+                over_rows(dot_tn(o[r], d1b[r][:, :part]) for r in every)[pad:],
+                over_rows(dot_tn(dqs[r], x_own[r]) for r in every)[:cols],
+            ],
+            0,
+        )
+        g_mix = shard_sum(own_mix, send_mix, 1)
+
+        d_vec = jnp.concatenate(
+            [over_rows(v) for v in zip(*d_vec1)] + [over_rows(v) for v in zip(*d_vec2)]
+        ).reshape(6, width)
         d_vec = d_vec + exchange(d_vec, "tp", n_tp, 1)
-        small = jnp.concatenate([d_bi, d_bq[:cols], d_bv])
-        if n_shard == 2:
-            send = jnp.concatenate([d_vec[:, part:].reshape(-1), small])
-            flat = jnp.concatenate([d_vec[:, :part].reshape(-1), small]) + exchange(send, "shard", 2, 1)
+        small = jnp.concatenate([over_rows(d_bi), over_rows(biases)[:cols], over_rows(d_bv)])
+        send_kv = over_rows(dot_tn(x_send[r], dkvs[r]) for r in every)
+        own_kv = over_rows(dot_tn(x_own[r], dkvs[r]) for r in every)
+        if n_shard == 2 and ctx_whole:
+            own_flat = jnp.concatenate([d_vec[:, :part].reshape(-1), small])
+            send_flat = jnp.concatenate([d_vec[:, part:].reshape(-1), small])
+            unit = 16 * n_ctx
+            lines = -(-own_flat.size // packed)
+            lines = lines + (-(part + lines)) % unit
+            fill = lines * packed - own_flat.size
+            own_flat = jnp.pad(own_flat, (0, fill)).reshape(lines, packed)
+            send_flat = jnp.pad(send_flat, (0, fill)).reshape(lines, packed)
+            own_kv = jnp.concatenate([own_kv, own_flat], 0)
+            send_kv = jnp.concatenate([send_kv.astype(BF), send_flat.astype(BF)], 0)
+            g_kv = ctx_sum(shard_sum(own_kv, send_kv, 0))
+            flat = g_kv[part:].reshape(-1)
+            g_kv = g_kv[:part]
         else:
             vec = lax.psum_scatter(unrolled(d_vec, 1), "shard", scatter_dimension=1, tiled=True)
             flat = jnp.concatenate([vec.reshape(-1), lax.psum(small, "shard")])
-        if n_ctx & (n_ctx - 1):
             flat = lax.psum(flat, "ctx")
-        else:
-            for bit in [1 << i for i in range(n_ctx.bit_length() - 1)]:
-                flat = flat + exchange(flat, "ctx", n_ctx, bit)
+            g_kv = ctx_sum(shard_sum(own_kv, send_kv, 0))
         vec = flat[: 6 * part].reshape(6, part)
         small = flat[6 * part :]
+
+        g_outer = ctx_sum(g_outer)
+        g_in = ctx_sum(g_in)
+        g_mix = ctx_sum(g_mix)
+        grad_qkv = jnp.concatenate([g_mix[cols:].T[:, None], g_kv.reshape(part, 2, cols)], 1)
+
+        hidden_grads = []
+        for r in every:
+            send = dot_nt(other_half(dqs[r]), w_q) + dot_nt(other_half(dkvs[r]), w_kv)
+            own = dot_nt(own_half(dqs[r]), w_q) + dot_nt(own_half(dkvs[r]), w_kv)
+            total = chip_sum(core_sum(own, send))
+            grad = (unrolled(dh1[r], 1) + total).astype(BF)
+            hidden_grads.append(in_order(both_halves(grad)))
+        outputs = [in_order(both_halves(unrolled(result[r], 1))) for r in every]
+
         return (
             jnp.stack(outputs),
             jnp.stack(hidden_grads),
             grad_qkv,
-            small[units:].reshape(2, cols),
-            g_out,
+            small[units : units + packed].reshape(2, cols),
+            g_mix[:cols],
             vec[0],
             vec[1],
             vec[2],

time: 407 us -> 352 us (0.86)
  waiting for transfers between devices: 136 us -> 107 us
  starting transfers between devices: 116 us -> 94.4 us
  other arithmetic: 38.2 us -> 24.4 us
  Pallas kernels: 30.9 us -> 38.5 us
  local copies, waits for them, and re-layouts: 20.9 us -> 25.6 us
    ppermute x76 -> x68, waiting for transfers between devices: 136 us -> 107 us  [the longest x60 107 us: exchange(): lax.ppermute(value, axis, [(i, i ^ bit) for i in range(size) if i ^ bit <...]
    ppermute x76 -> x68, starting transfers between devices: 116 us -> 94.4 us  [the longest x60 86.9 us: exchange(): lax.ppermute(value, axis, [(i, i ^ bit) for i in range(size) if i ^ bit <...]
    dot_general x20, matrix products: 14.4 us -> 25.5 us  [dot_tn(): lax.dot_general(a, b, (((0,), (0,)), ((), ())), preferred_element_type=F32)]
    pallas_call x4, Pallas kernels: 30.9 us -> 38.5 us  [the longest x2 22.4 us: stage4(): attend_bwd(ranges[r], q[r], q_seg3[r], key_col[r], o[r], do, lse[r], *kv[r])]
    dot_general x16, matrix products: 22.6 us -> 15.3 us  [dot_nt(): lax.dot_general(a, b, (((1,), (1,)), ((), ())), preferred_element_type=F32)]
    another operation x21 -> x1, local copies, waits for them, and re-layouts: 6.32 us -> 0.08 us  [body(): places = jnp.broadcast_to(jnp.stack(places)[None], (rows, slots))]
    unnamed x148 -> x209, local copies, waits for them, and re-layouts: 4.11 us -> 8.88 us
    convert_element_type x17 -> x16, other arithmetic: 8.17 us -> 5.8 us  [the longest x4 2.45 us: body(): (p.astype(F32) + c.astype(F32)).astype(BF)]
  transfers between devices with their start and end apart: 76 -> 68, of which waited for: 32 -> 26; matrix products, arithmetic and copies ran while one was open for 24% -> 26% of each run, Pallas kernels for 8% -> 11%
where the time goes in v2:
time: 352 us; the launch traced here: 347 us
  waiting for transfers between devices  107 us (30%)
  starting transfers between devices  94.4 us (27%)
  matrix products  54.6 us (16%)
  Pallas kernels  38.5 us (11%)
  local copies, waits for them, and re-layouts  25.6 us (7%)
  other arithmetic  24.4 us (7%)
    ppermute x60, waiting for transfers between devices, exchange(): lax.ppermute(value, axis, [(i, i ^ bit) for i in range(size) if i ^ bit <...  107 us
    ppermute x60, starting transfers between devices, exchange(): lax.ppermute(value, axis, [(i, i ^ bit) for i in range(size) if i ^ bit <...  86.9 us
    dot_general x20, matrix products, dot_tn(): lax.dot_general(a, b, (((0,), (0,)), ((), ())), preferred_element_type=F32)  25.5 us
    pallas_call x2, Pallas kernels, stage4(): attend_bwd(ranges[r], q[r], q_seg3[r], key_col[r], o[r], do, lse[r], *kv[r])  22.4 us
    pallas_call x2, Pallas kernels, stage1(): attend_fwd(ranges[r], gated(q[r], gate), q_seg3[r], key_col[r], *kv[r])  16.1 us
    dot_general x16, matrix products, dot_nt(): lax.dot_general(a, b, (((1,), (1,)), ((), ())), preferred_element_type=F32)  15.3 us
    dot_general x14, matrix products, dot(): return jnp.dot(a, b, preferred_element_type=F32)  13.8 us
    unnamed x209, local copies, waits for them, and re-layouts  8.88 us
  transfers between devices with their start and end apart: 68, of which 26 were waited for; matrix products, arithmetic and copies ran while one was open for 26% of the time, Pallas kernels for 11%

profile of v2, /device:TPU:0, one launch (start us, length us, event | category | flops | bytes accessed | tf_op | source)
XLA Modules:
  0.0 347.4 jit_solution(5678689750215407125)
XLA Ops:
  1.9 3.0 collective-permute-start.1
  15.3 5.0 %collective-permute-start.2 = (bf16[512,384]{1,0:T(8,128)(2,1)S(1)}, bf16[512,384]{1,0:T(8,128)(2,1)S(1)}, u32[]{:S(2)}, u32[]{:S(2)}) collective-permute-start(bf16[512,384]{1,0:T(8,128)(2,1)S(1)} %fusion.30.rest_0_), channel_id=1, source_target_pairs={{0,4},{4,0},{8,12},{12,8},{1,5},{5,1},{9,13},{13,9},{2,6},{6,2},{1... | collective-permute-start | bytes 1179656 | tf_op jit(solution)/shard_map/ppermute | solution.py:228
  21.4 6.3 %collective-permute-start.4 = (bf16[512,384]{1,0:T(8,128)(2,1)S(1)}, bf16[512,384]{1,0:T(8,128)(2,1)S(1)}, u32[]{:S(2)}, u32[]{:S(2)}) collective-permute-start(bf16[512,384]{1,0:T(8,128)(2,1)S(1)} %collective-permute-done.3.rest_2_), channel_id=1, source_target_pairs={{0,4},{4,0},{8,12},{12,8},{1,5},{5,1},{9,13},{13,9},{2,6},{6,2},{1... | collective-permute-start | bytes 1179656 | tf_op jit(solution)/shard_map/ppermute | solution.py:228
  31.8 3.2 collective-permute-done.6
  36.5 5.5 %collective-permute-start.9 = (bf16[512,384]{1,0:T(8,128)(2,1)S(1)}, bf16[512,384]{1,0:T(8,128)(2,1)}, u32[]{:S(2)}, u32[]{:S(2)}) collective-permute-start(bf16[512,384]{1,0:T(8,128)(2,1)S(1)} %fusion.29.rest_0_), channel_id=1, source_target_pairs={{0,4},{4,0},{8,12},{12,8},{1,5},{5,1},{9,13},{13,9},{2,6},{6,2},{1... | collective-permute-start | bytes 1179656 | tf_op jit(solution)/shard_map/ppermute | solution.py:228
  42.1 7.0 %attend_forward.2 = (bf16[512,256]{1,0:T(8,128)(2,1)S(1)}, f32[2,1,768]{2,1,0:T(1,128)S(1)}) custom-call(s32[11]{0:T(128)S(1)} %get-tuple-element.179.rng, bf16[512,256]{1,0:T(8,128)(2,1)S(1)} %fusion.35.q_ref, s32[2,1,768]{2,1,0:T(1,128)S(1)} %tile.16.qseg_ref, s32[2560,1]{1,0:T(8,128)S(1)} %copy.69.kseg_ref, bf16[512,384]{1,0:T(8,128)(2,1)S(1)} %fusion.30.rest_0_, ...), custom_call_target="tpu_custom_call" | custom-call | flops 3019898880 | bytes 1966080 | tf_op jit(solution)/shard_map/attend_forward/pallas_call | solution.py:438
  60.9 5.1 %collective-permute-done.11.rest_3_ = bf16[512,384]{1,0:T(8,128)(2,1)S(1)} collective-permute-done((bf16[512,384]{1,0:T(8,128)(2,1)}, bf16[512,384]{1,0:T(8,128)(2,1)S(1)}, u32[]{:S(2)}, u32[]{:S(2)}) %collective-permute-start.11) | collective-permute-done | bytes 393248 | tf_op jit(solution)/shard_map/ppermute | solution.py:228
  66.0 9.1 %attend_forward.3 = (bf16[512,256]{1,0:T(8,128)(2,1)S(1)}, f32[2,1,768]{2,1,0:T(1,128)S(1)}) custom-call(s32[11]{0:T(128)S(1)} %get-tuple-element.180.rng, bf16[512,256]{1,0:T(8,128)(2,1)S(1)} %fusion.36.q_ref, s32[2,1,768]{2,1,0:T(1,128)S(1)} %tile.17.qseg_ref, s32[2560,1]{1,0:T(8,128)S(1)} %copy.73.kseg_ref, bf16[512,384]{1,0:T(8,128)(2,1)S(1)} %fusion.29.rest_0_, ...), custom_call_target="tpu_custom_call" | custom-call | flops 3019898880 | bytes 1966080 | tf_op jit(solution)/shard_map/attend_forward/pallas_call | solution.py:438
  76.5 3.8 %collective-permute-start.15 = (bf16[384,768]{1,0:T(8,128)(2,1)S(1)}, bf16[384,768]{1,0:T(8,128)(2,1)S(1)}, u32[]{:S(2)}, u32[]{:S(2)}) collective-permute-start(bf16[384,768]{1,0:T(8,128)(2,1)S(1)} %convert_element_type.420), channel_id=1, source_target_pairs={{0,16},{16,0},{1,17},{17,1},{2,18},{18,2},{3,19},{19,3},{4,20},{20... | collective-permute-start | bytes 1769480 | tf_op jit(solution)/shard_map/ppermute | solution.py:228
  84.9 9.6 %collective-permute-done.15 = bf16[384,768]{1,0:T(8,128)(2,1)S(1)} collective-permute-done((bf16[384,768]{1,0:T(8,128)(2,1)S(1)}, bf16[384,768]{1,0:T(8,128)(2,1)S(1)}, u32[]{:S(2)}, u32[]{:S(2)}) %collective-permute-start.15) | collective-permute-done | bytes 589856 | tf_op jit(solution)/shard_map/ppermute | solution.py:228
  96.6 9.8 %collective-permute-done.16 = bf16[768,384]{1,0:T(8,128)(2,1)S(1)} collective-permute-done((bf16[768,384]{1,0:T(8,128)(2,1)S(1)}, bf16[768,384]{1,0:T(8,128)(2,1)S(1)}, u32[]{:S(2)}, u32[]{:S(2)}) %collective-permute-start.16) | collective-permute-done | bytes 589856 | tf_op jit(solution)/shard_map/ppermute | solution.py:228
  118.6 7.1 %collective-permute-done.18 = bf16[256,768]{1,0:T(8,128)(2,1)S(1)} collective-permute-done((bf16[256,768]{1,0:T(8,128)(2,1)S(1)}, bf16[256,768]{1,0:T(8,128)(2,1)S(1)}, u32[]{:S(2)}, u32[]{:S(2)}) %collective-permute-start.18) | collective-permute-done | bytes 393248 | tf_op jit(solution)/shard_map/ppermute | solution.py:228
  133.4 3.2 collective-permute-done.23
  163.2 10.7 %attend_backward.2 = (bf16[512,256]{1,0:T(8,128)(2,1)S(1)}, f32[1,256]{1,0:T(1,128)S(1)}, bf16[512,384]{1,0:T(8,128)(2,1)S(1)}, bf16[512,384]{1,0:T(8,128)(2,1)S...) custom-call(s32[11]{0:T(128)S(1)} %get-tuple-element.179.rng, ...), custom_call_target="tpu_custom_call" | custom-call | flops 9059696640 | bytes 3932160 | tf_op jit(solution)/shard_map/attend_backward/pallas_call | solution.py:499
  178.7 3.4 collective-permute-start.31
  197.3 11.7 %attend_backward.3 = (bf16[512,256]{1,0:T(8,128)(2,1)S(1)}, f32[1,256]{1,0:T(1,128)S(1)}, bf16[512,384]{1,0:T(8,128)(2,1)S(1)}, bf16[512,384]{1,0:T(8,128)(2,1)S...) custom-call(s32[11]{0:T(128)S(1)} %get-tuple-element.180.rng, ...), custom_call_target="tpu_custom_call" | custom-call | flops 9059696640 | bytes 3932160 | tf_op jit(solution)/shard_map/attend_backward/pallas_call | solution.py:499
  210.9 5.0 %collective-permute-start.47 = (bf16[384,384]{1,0:T(8,128)(2,1)S(1)}, bf16[384,384]{1,0:T(8,128)(2,1)S(1)}, u32[]{:S(2)}, u32[]{:S(2)}) collective-permute-start(bf16[384,384]{1,0:T(8,128)(2,1)S(1)} %pad_maximum_fusion.19), channel_id=1, source_target_pairs={{0,16},{16,0},{1,17},{17,1},{2,18},{18,2},{3,19},{19,3},{4,20},{20... | collective-permute-start | bytes 884744 | tf_op jit(solution)/shard_map/ppermute | solution.py:228
  219.3 4.1 %collective-permute-start.34 = (bf16[512,384]{1,0:T(8,128)(2,1)S(1)}, bf16[512,384]{1,0:T(8,128)(2,1)S(1)}, u32[]{:S(2)}, u32[]{:S(2)}) collective-permute-start(bf16[512,384]{1,0:T(8,128)(2,1)S(1)} %add_convert_fusion.2), channel_id=1, source_target_pairs={{0,4},{4,0},{8,12},{12,8},{1,5},{5,1},{9,13},{13,9},{2,6},{6,2},{1... | collective-permute-start | bytes 1179656 | tf_op jit(solution)/shard_map/ppermute | solution.py:228
  226.6 15.5 %collective-permute-done.65 = bf16[192,384]{1,0:T(8,128)(2,1)S(1)} collective-permute-done((bf16[192,384]{1,0:T(8,128)(2,1)S(1)}, bf16[192,384]{1,0:T(8,128)(2,1)S(1)}, u32[]{:S(2)}, u32[]{:S(2)}) %collective-permute-start.65) | collective-permute-done | bytes 147488 | tf_op jit(solution)/shard_map/ppermute | solution.py:228
  242.1 3.5 %collective-permute-start.60 = (bf16[96,768]{1,0:T(8,128)(2,1)S(1)}, bf16[96,768]{1,0:T(8,128)(2,1)S(1)}, u32[]{:S(2)}, u32[]{:S(2)}) collective-permute-start(bf16[96,768]{1,0:T(8,128)(2,1)S(1)} %dynamic-slice_convert_fusion.4), channel_id=1, source_target_pairs={{0,8},{4,12},{8,0},{12,4},{1,9},{5,13},{9,1},{13,5},{2,10},{6,14},... | collective-permute-start | bytes 442376 | tf_op jit(solution)/shard_map/ppermute | solution.py:228
  245.6 4.7 %collective-permute-done.60 = bf16[96,768]{1,0:T(8,128)(2,1)S(1)} collective-permute-done((bf16[96,768]{1,0:T(8,128)(2,1)S(1)}, bf16[96,768]{1,0:T(8,128)(2,1)S(1)}, u32[]{:S(2)}, u32[]{:S(2)}) %collective-permute-start.60) | collective-permute-done | bytes 147488 | tf_op jit(solution)/shard_map/ppermute | solution.py:228
  253.4 6.5 %collective-permute-done.66 = bf16[192,384]{1,0:T(8,128)(2,1)S(1)} collective-permute-done((bf16[192,384]{1,0:T(8,128)(2,1)S(1)}, bf16[192,384]{1,0:T(8,128)(2,1)S(1)}, u32[]{:S(2)}, u32[]{:S(2)}) %collective-permute-start.66) | collective-permute-done | bytes 147488 | tf_op jit(solution)/shard_map/ppermute | solution.py:228
  260.7 4.0 %collective-permute-done.61 = bf16[96,768]{1,0:T(8,128)(2,1)S(1)} collective-permute-done((bf16[96,768]{1,0:T(8,128)(2,1)S(1)}, bf16[96,768]{1,0:T(8,128)(2,1)S(1)}, u32[]{:S(2)}, u32[]{:S(2)}) %collective-permute-start.61) | collective-permute-done | bytes 147488 | tf_op jit(solution)/shard_map/ppermute | solution.py:228
  266.9 5.0 %collective-permute-start.62 = (bf16[192,768]{1,0:T(8,128)(2,1)S(1)}, bf16[192,768]{1,0:T(8,128)(2,1)S(1)}, u32[]{:S(2)}, u32[]{:S(2)}) collective-permute-start(bf16[192,768]{1,0:T(8,128)(2,1)S(1)} %maximum_select_fusion.18), channel_id=1, source_target_pairs={{0,4},{4,0},{8,12},{12,8},{1,5},{5,1},{9,13},{13,9},{2,6},{6,2},{1... | collective-permute-start | bytes 884744 | tf_op jit(solution)/shard_map/ppermute | solution.py:228
  273.1 2.8 collective-permute-start.43
  279.9 7.5 %collective-permute-done.49 = bf16[96,384]{1,0:T(8,128)(2,1)S(1)} collective-permute-done((bf16[96,384]{1,0:T(8,128)(2,1)S(1)}, bf16[96,384]{1,0:T(8,128)(2,1)S(1)}, u32[]{:S(2)}, u32[]{:S(2)}) %collective-permute-start.49) | collective-permute-done | bytes 73760 | tf_op jit(solution)/shard_map/ppermute | solution.py:228
  287.4 3.4 collective-permute-start.50
  291.1 2.9 collective-permute-done.50
  294.0 2.7 collective-permute-start.51
  325.5 3.0 collective-permute-done.55
  329.8 5.2 %collective-permute-done.56 = bf16[112,384]{1,0:T(8,128)(2,1)S(1)} collective-permute-done((bf16[112,384]{1,0:T(8,128)(2,1)S(1)}, bf16[112,384]{1,0:T(8,128)(2,1)S(1)}, u32[]{:S(2)}, u32[]{:S(2)}) %collective-permute-start.56) | collective-permute-done | bytes 86048 | tf_op jit(solution)/shard_map/ppermute | solution.py:228
  336.2 5.1 %collective-permute-done.57 = bf16[224,384]{1,0:T(8,128)(2,1)S(1)} collective-permute-done((bf16[224,384]{1,0:T(8,128)(2,1)S(1)}, bf16[224,384]{1,0:T(8,128)(2,1)S(1)}, u32[]{:S(2)}, u32[]{:S(2)}) %collective-permute-start.57) | collective-permute-done | bytes 172064 | tf_op jit(solution)/shard_map/ppermute | solution.py:228
  (556 shorter events, 159.7 us)
Async XLA Ops:
  5.9 14.4 %collective-permute-start = (bf16[384,256]{0,1:T(8,128)(2,1)S(1)}, bf16[384,256]{0,1:T(8,128)(2,1)S(1)}, u32[]{:S(2)}, u32[]{:S(2)}) collective-permute-start(bf16[384,256]{0,1:T(8,128)(2,1)S(1)} %pad.23), channel_id=1, source_target_pairs={{0,16},{16,0},{1,17},{17,1},{2,18},{18,2},{3,19},{19,3},{4,20},{20... | collective-permute-start | bytes 589832 | tf_op jit(solution)/shard_map/ppermute | solution.py:228
  15.3 13.6 %collective-permute-start.2 = (bf16[512,384]{1,0:T(8,128)(2,1)S(1)}, bf16[512,384]{1,0:T(8,128)(2,1)S(1)}, u32[]{:S(2)}, u32[]{:S(2)}) collective-permute-start(bf16[512,384]{1,0:T(8,128)(2,1)S(1)} %fusion.30.rest_0_), channel_id=1, source_target_pairs={{0,4},{4,0},{8,12},{12,8},{1,5},{5,1},{9,13},{13,9},{2,6},{6,2},{1... | collective-permute-start | bytes 1179656 | tf_op jit(solution)/shard_map/ppermute | solution.py:228
  21.4 20.7 %collective-permute-start.4 = (bf16[512,384]{1,0:T(8,128)(2,1)S(1)}, bf16[512,384]{1,0:T(8,128)(2,1)S(1)}, u32[]{:S(2)}, u32[]{:S(2)}) collective-permute-start(bf16[512,384]{1,0:T(8,128)(2,1)S(1)} %collective-permute-done.3.rest_2_), channel_id=1, source_target_pairs={{0,4},{4,0},{8,12},{12,8},{1,5},{5,1},{9,13},{13,9},{2,6},{6,2},{1... | collective-permute-start | bytes 1179656 | tf_op jit(solution)/shard_map/ppermute | solution.py:228
  28.9 13.1 %collective-permute-start.5 = (bf16[512,384]{1,0:T(8,128)(2,1)S(1)}, bf16[512,384]{1,0:T(8,128)(2,1)S(1)}, u32[]{:S(2)}, u32[]{:S(2)}) collective-permute-start(bf16[512,384]{1,0:T(8,128)(2,1)S(1)} %collective-permute-done.2.rest_1_), channel_id=1, source_target_pairs={{4,8},{8,4},{5,9},{9,5},{6,10},{10,6},{7,11},{11,7},{20,24},{24,20... | collective-permute-start | bytes 1179656 | tf_op jit(solution)/shard_map/ppermute | solution.py:237
  35.1 19.2 %collective-permute-start.10 = (bf16[512,384]{1,0:T(8,128)(2,1)S(1)}, bf16[512,384]{1,0:T(8,128)(2,1)}, u32[]{:S(2)}, u32[]{:S(2)}) collective-permute-start(bf16[512,384]{1,0:T(8,128)(2,1)S(1)} %fusion.29.rest_0_), channel_id=1, source_target_pairs={{4,8},{8,4},{5,9},{9,5},{6,10},{10,6},{7,11},{11,7},{20,24},{24,20... | collective-permute-start | bytes 1179656 | tf_op jit(solution)/shard_map/ppermute | solution.py:237
  36.5 19.3 %collective-permute-start.9 = (bf16[512,384]{1,0:T(8,128)(2,1)S(1)}, bf16[512,384]{1,0:T(8,128)(2,1)}, u32[]{:S(2)}, u32[]{:S(2)}) collective-permute-start(bf16[512,384]{1,0:T(8,128)(2,1)S(1)} %fusion.29.rest_0_), channel_id=1, source_target_pairs={{0,4},{4,0},{8,12},{12,8},{1,5},{5,1},{9,13},{13,9},{2,6},{6,2},{1... | collective-permute-start | bytes 1179656 | tf_op jit(solution)/shard_map/ppermute | solution.py:228
  59.3 21.1 %collective-permute-start.8 = (bf16[256,768]{1,0:T(8,128)(2,1)S(1)}, bf16[256,768]{1,0:T(8,128)(2,1)S(1)}, u32[]{:S(2)}, u32[]{:S(2)}) collective-permute-start(bf16[256,768]{1,0:T(8,128)(2,1)S(1)} %fusion.17), channel_id=1, source_target_pairs={{0,2},{1,3},{2,0},{3,1},{4,6},{5,7},{6,4},{7,5},{8,10},{9,11},{10,... | collective-permute-start | bytes 1179656 | tf_op jit(solution)/shard_map/ppermute | solution.py:228
  76.5 18.0 %collective-permute-start.15 = (bf16[384,768]{1,0:T(8,128)(2,1)S(1)}, bf16[384,768]{1,0:T(8,128)(2,1)S(1)}, u32[]{:S(2)}, u32[]{:S(2)}) collective-permute-start(bf16[384,768]{1,0:T(8,128)(2,1)S(1)} %convert_element_type.420), channel_id=1, source_target_pairs={{0,16},{16,0},{1,17},{17,1},{2,18},{18,2},{3,19},{19,3},{4,20},{20... | collective-permute-start | bytes 1769480 | tf_op jit(solution)/shard_map/ppermute | solution.py:228
  81.5 13.0 %collective-permute-start.14 = (bf16[256,768]{1,0:T(8,128)(2,1)S(1)}, bf16[256,768]{1,0:T(8,128)(2,1)S(1)}, u32[]{:S(2)}, u32[]{:S(2)}) collective-permute-start(bf16[256,768]{1,0:T(8,128)(2,1)S(1)} %fusion.55), channel_id=1, source_target_pairs={{0,1},{1,0},{2,3},{3,2},{4,5},{5,4},{6,7},{7,6},{8,9},{9,8},{10,11... | collective-permute-start | bytes 1179656 | tf_op jit(solution)/shard_map/ppermute | solution.py:228
  82.8 23.6 %collective-permute-start.16 = (bf16[768,384]{1,0:T(8,128)(2,1)S(1)}, bf16[768,384]{1,0:T(8,128)(2,1)S(1)}, u32[]{:S(2)}, u32[]{:S(2)}) collective-permute-start(bf16[768,384]{1,0:T(8,128)(2,1)S(1)} %convert_element_type.422), channel_id=1, source_target_pairs={{0,16},{16,0},{1,17},{17,1},{2,18},{18,2},{3,19},{19,3},{4,20},{20... | collective-permute-start | bytes 1769480 | tf_op jit(solution)/shard_map/ppermute | solution.py:228
  83.4 23.6 %collective-permute-start.19 = (bf16[256,768]{1,0:T(8,128)(2,1)S(1)}, bf16[256,768]{1,0:T(8,128)(2,1)S(1)}, u32[]{:S(2)}, u32[]{:S(2)}) collective-permute-start(bf16[256,768]{1,0:T(8,128)(2,1)S(1)} %fusion.19), channel_id=1, source_target_pairs={{0,2},{1,3},{2,0},{3,1},{4,6},{5,7},{6,4},{7,5},{8,10},{9,11},{10,... | collective-permute-start | bytes 1179656 | tf_op jit(solution)/shard_map/ppermute | solution.py:228
  151.1 25.0 %collective-permute-start.38 = (bf16[256,768]{1,0:T(8,128)(2,1)S(1)}, bf16[256,768]{1,0:T(8,128)(2,1)S(1)}, u32[]{:S(2)}, u32[]{:S(2)}) collective-permute-start(bf16[256,768]{1,0:T(8,128)(2,1)S(1)} %fusion.23), channel_id=1, source_target_pairs={{0,2},{1,3},{2,0},{3,1},{4,6},{5,7},{6,4},{7,5},{8,10},{9,11},{10,... | collective-permute-start | bytes 1179656 | tf_op jit(solution)/shard_map/ppermute | solution.py:228
  155.5 37.2 %collective-permute-start.58 = (bf16[384,768]{1,0:T(8,128)(2,1)}, bf16[384,768]{1,0:T(8,128)(2,1)}, u32[]{:S(2)}, u32[]{:S(2)}) collective-permute-start(bf16[384,768]{1,0:T(8,128)(2,1)} %fusion.12), channel_id=1, source_target_pairs={{0,16},{16,0},{1,17},{17,1},{2,18},{18,2},{3,19},{19,3},{4,20},{20... | collective-permute-start | bytes 1769480 | tf_op jit(solution)/shard_map/ppermute | solution.py:228
  161.1 28.2 %collective-permute-start.63 = (bf16[768,384]{1,0:T(8,128)(2,1)}, bf16[768,384]{1,0:T(8,128)(2,1)}, u32[]{:S(2)}, u32[]{:S(2)}) collective-permute-start(bf16[768,384]{1,0:T(8,128)(2,1)} %fusion.13), channel_id=1, source_target_pairs={{0,16},{16,0},{1,17},{17,1},{2,18},{18,2},{3,19},{19,3},{4,20},{20... | collective-permute-start | bytes 1769480 | tf_op jit(solution)/shard_map/ppermute | solution.py:228
  178.6 17.1 %collective-permute-start.39 = (bf16[256,768]{1,0:T(8,128)(2,1)}, bf16[256,768]{1,0:T(8,128)(2,1)}, u32[]{:S(2)}, u32[]{:S(2)}) collective-permute-start(bf16[256,768]{1,0:T(8,128)(2,1)} %convert_element_type.479), channel_id=1, source_target_pairs={{0,1},{1,0},{2,3},{3,2},{4,5},{5,4},{6,7},{7,6},{8,9},{9,8},{10,11... | collective-permute-start | bytes 1179656 | tf_op jit(solution)/shard_map/ppermute | solution.py:228
  178.7 37.3 %collective-permute-start.31 = (bf16[512,384]{1,0:T(8,128)(2,1)}, bf16[512,384]{1,0:T(8,128)(2,1)}, u32[]{:S(2)}, u32[]{:S(2)}) collective-permute-start(bf16[512,384]{1,0:T(8,128)(2,1)} %get-tuple-element.67), channel_id=1, source_target_pairs={{0,4},{4,0},{8,12},{12,8},{1,5},{5,1},{9,13},{13,9},{2,6},{6,2},{1... | collective-permute-start | bytes 1179656 | tf_op jit(solution)/shard_map/ppermute | solution.py:228
  187.5 30.5 %collective-permute-start.33 = (bf16[512,384]{1,0:T(8,128)(2,1)}, bf16[512,384]{1,0:T(8,128)(2,1)}, u32[]{:S(2)}, u32[]{:S(2)}) collective-permute-start(bf16[512,384]{1,0:T(8,128)(2,1)} %get-tuple-element.69), channel_id=1, source_target_pairs={{4,8},{8,4},{5,9},{9,5},{6,10},{10,6},{7,11},{11,7},{20,24},{24,20... | collective-permute-start | bytes 1179656 | tf_op jit(solution)/shard_map/ppermute | solution.py:237
  191.9 32.9 %collective-permute-start.64 = (bf16[384,384]{1,0:T(8,128)(2,1)S(1)}, bf16[384,384]{1,0:T(8,128)(2,1)S(1)}, u32[]{:S(2)}, u32[]{:S(2)}) collective-permute-start(bf16[384,384]{1,0:T(8,128)(2,1)S(1)} %dynamic-slice_convert_fusion), channel_id=1, source_target_pairs={{0,4},{4,0},{8,12},{12,8},{1,5},{5,1},{9,13},{13,9},{2,6},{6,2},{1... | collective-permute-start | bytes 884744 | tf_op jit(solution)/shard_map/ppermute | solution.py:228
  194.4 30.6 %collective-permute-start.59 = (bf16[192,768]{1,0:T(8,128)(2,1)S(1)}, bf16[192,768]{1,0:T(8,128)(2,1)S(1)}, u32[]{:S(2)}, u32[]{:S(2)}) collective-permute-start(bf16[192,768]{1,0:T(8,128)(2,1)S(1)} %dynamic-slice_convert_fusion.1), channel_id=1, source_target_pairs={{0,4},{4,0},{8,12},{12,8},{1,5},{5,1},{9,13},{13,9},{2,6},{6,2},{1... | collective-permute-start | bytes 884744 | tf_op jit(solution)/shard_map/ppermute | solution.py:228
  210.9 41.1 %collective-permute-start.47 = (bf16[384,384]{1,0:T(8,128)(2,1)S(1)}, bf16[384,384]{1,0:T(8,128)(2,1)S(1)}, u32[]{:S(2)}, u32[]{:S(2)}) collective-permute-start(bf16[384,384]{1,0:T(8,128)(2,1)S(1)} %pad_maximum_fusion.19), channel_id=1, source_target_pairs={{0,16},{16,0},{1,17},{17,1},{2,18},{18,2},{3,19},{19,3},{4,20},{20... | collective-permute-start | bytes 884744 | tf_op jit(solution)/shard_map/ppermute | solution.py:228
  217.0 55.0 %collective-permute-start.32 = (bf16[512,384]{1,0:T(8,128)(2,1)S(1)}, bf16[512,384]{1,0:T(8,128)(2,1)S(1)}, u32[]{:S(2)}, u32[]{:S(2)}) collective-permute-start(bf16[512,384]{1,0:T(8,128)(2,1)S(1)} %add_convert_fusion.3), channel_id=1, source_target_pairs={{4,8},{8,4},{5,9},{9,5},{6,10},{10,6},{7,11},{11,7},{20,24},{24,20... | collective-permute-start | bytes 1179656 | tf_op jit(solution)/shard_map/ppermute | solution.py:237
  219.3 53.9 %collective-permute-start.34 = (bf16[512,384]{1,0:T(8,128)(2,1)S(1)}, bf16[512,384]{1,0:T(8,128)(2,1)S(1)}, u32[]{:S(2)}, u32[]{:S(2)}) collective-permute-start(bf16[512,384]{1,0:T(8,128)(2,1)S(1)} %add_convert_fusion.2), channel_id=1, source_target_pairs={{0,4},{4,0},{8,12},{12,8},{1,5},{5,1},{9,13},{13,9},{2,6},{6,2},{1... | collective-permute-start | bytes 1179656 | tf_op jit(solution)/shard_map/ppermute | solution.py:228
  224.8 39.9 %collective-permute-start.40 = (bf16[512,384]{1,0:T(8,128)(2,1)S(1)}, bf16[512,384]{1,0:T(8,128)(2,1)S(1)}, u32[]{:S(2)}, u32[]{:S(2)}) collective-permute-start(bf16[512,384]{1,0:T(8,128)(2,1)S(1)} %get-tuple-element.75), channel_id=1, source_target_pairs={{0,4},{4,0},{8,12},{12,8},{1,5},{5,1},{9,13},{13,9},{2,6},{6,2},{1... | collective-permute-start | bytes 1179656 | tf_op jit(solution)/shard_map/ppermute | solution.py:228
  225.0 17.1 %collective-permute-start.65 = (bf16[192,384]{1,0:T(8,128)(2,1)S(1)}, bf16[192,384]{1,0:T(8,128)(2,1)S(1)}, u32[]{:S(2)}, u32[]{:S(2)}) collective-permute-start(bf16[192,384]{1,0:T(8,128)(2,1)S(1)} %dynamic-slice_convert_fusion.3), channel_id=1, source_target_pairs={{0,8},{4,12},{8,0},{12,4},{1,9},{5,13},{9,1},{13,5},{2,10},{6,14},... | collective-permute-start | bytes 442376 | tf_op jit(solution)/shard_map/ppermute | solution.py:228
  252.0 12.7 %collective-permute-start.61 = (bf16[96,768]{1,0:T(8,128)(2,1)S(1)}, bf16[96,768]{1,0:T(8,128)(2,1)S(1)}, u32[]{:S(2)}, u32[]{:S(2)}) collective-permute-start(bf16[96,768]{1,0:T(8,128)(2,1)S(1)} %add_convert_fusion.7), channel_id=1, source_target_pairs={{0,8},{4,12},{8,0},{12,4},{1,9},{5,13},{9,1},{13,5},{2,10},{6,14},... | collective-permute-start | bytes 442376 | tf_op jit(solution)/shard_map/ppermute | solution.py:228
  264.6 13.6 %collective-permute-start.48 = (bf16[192,384]{1,0:T(8,128)(2,1)S(1)}, bf16[192,384]{1,0:T(8,128)(2,1)S(1)}, u32[]{:S(2)}, u32[]{:S(2)}) collective-permute-start(bf16[192,384]{1,0:T(8,128)(2,1)S(1)} %dynamic-slice_convert_fusion.5), channel_id=1, source_target_pairs={{0,4},{4,0},{8,12},{12,8},{1,5},{5,1},{9,13},{13,9},{2,6},{6,2},{1... | collective-permute-start | bytes 442376 | tf_op jit(solution)/shard_map/ppermute | solution.py:228
  264.7 29.3 %collective-permute-start.67 = (bf16[384,384]{1,0:T(8,128)(2,1)S(1)}, bf16[384,384]{1,0:T(8,128)(2,1)S(1)}, u32[]{:S(2)}, u32[]{:S(2)}) collective-permute-start(bf16[384,384]{1,0:T(8,128)(2,1)S(1)} %maximum_select_fusion.19), channel_id=1, source_target_pairs={{0,4},{4,0},{8,12},{12,8},{1,5},{5,1},{9,13},{13,9},{2,6},{6,2},{1... | collective-permute-start | bytes 884744 | tf_op jit(solution)/shard_map/ppermute | solution.py:228
  266.9 30.9 %collective-permute-start.62 = (bf16[192,768]{1,0:T(8,128)(2,1)S(1)}, bf16[192,768]{1,0:T(8,128)(2,1)S(1)}, u32[]{:S(2)}, u32[]{:S(2)}) collective-permute-start(bf16[192,768]{1,0:T(8,128)(2,1)S(1)} %maximum_select_fusion.18), channel_id=1, source_target_pairs={{0,4},{4,0},{8,12},{12,8},{1,5},{5,1},{9,13},{13,9},{2,6},{6,2},{1... | collective-permute-start | bytes 884744 | tf_op jit(solution)/shard_map/ppermute | solution.py:228
  272.1 29.2 %collective-permute-start.41 = (bf16[512,384]{1,0:T(8,128)(2,1)S(1)}, bf16[512,384]{1,0:T(8,128)(2,1)S(1)}, u32[]{:S(2)}, u32[]{:S(2)}) collective-permute-start(bf16[512,384]{1,0:T(8,128)(2,1)S(1)} %add_convert_fusion.1), channel_id=1, source_target_pairs={{4,8},{8,4},{5,9},{9,5},{6,10},{10,6},{7,11},{11,7},{20,24},{24,20... | collective-permute-start | bytes 1179656 | tf_op jit(solution)/shard_map/ppermute | solution.py:237
  273.1 28.2 %collective-permute-start.43 = (bf16[512,384]{1,0:T(8,128)(2,1)S(1)}, bf16[512,384]{1,0:T(8,128)(2,1)S(1)}, u32[]{:S(2)}, u32[]{:S(2)}) collective-permute-start(bf16[512,384]{1,0:T(8,128)(2,1)S(1)} %add_convert_fusion), channel_id=1, source_target_pairs={{0,4},{4,0},{8,12},{12,8},{1,5},{5,1},{9,13},{13,9},{2,6},{6,2},{1... | collective-permute-start | bytes 1179656 | tf_op jit(solution)/shard_map/ppermute | solution.py:228
  310.1 12.9 %collective-permute-start.44 = (bf16[256,768]{1,0:T(8,128)(2,1)}, bf16[256,768]{1,0:T(8,128)(2,1)}, u32[]{:S(2)}, u32[]{:S(2)}) collective-permute-start(bf16[256,768]{1,0:T(8,128)(2,1)} %fusion.27), channel_id=1, source_target_pairs={{0,1},{1,0},{2,3},{3,2},{4,5},{5,4},{6,7},{7,6},{8,9},{9,8},{10,11... | collective-permute-start | bytes 1179656 | tf_op jit(solution)/shard_map/ppermute | solution.py:228
  320.6 15.3 %collective-permute-start.37 = (bf16[256,768]{1,0:T(8,128)(2,1)S(1)}, bf16[256,768]{1,0:T(8,128)(2,1)S(1)}, u32[]{:S(2)}, u32[]{:S(2)}) collective-permute-start(bf16[256,768]{1,0:T(8,128)(2,1)S(1)} %fusion.52), channel_id=1, source_target_pairs={{0,1},{1,0},{2,3},{3,2},{4,5},{5,4},{6,7},{7,6},{8,9},{9,8},{10,11... | collective-permute-start | bytes 1179656 | tf_op jit(solution)/shard_map/ppermute | solution.py:228
  (138 other events, 1091.2 us)
